TPU v7x, 32 devices: a whole 2x2x4 slice. The times are simulated.
32 devices in a mesh: dp: 8 (over z, x), mp: 4 (over y, core).
Axes of the slice: x: 2, y: 2, z: 4, core: 2. Of those that a mesh axis runs over, the one named last changes fastest.
Arguments:
- patches: bfloat16 [8, 2048, 768], P('dp'), may hold values from -6 to 6
- cotangent: bfloat16 [8, 2048, 768], P('dp'), may hold values from -6 to 6
- keep_mask: int32 [8, 2048], P('dp'), may hold values from 0 to 1, as said below
- segment_ids: int32 [8, 2048], P('dp'), may hold values from 0 to 7, never falling along the last dimension, each value on 1 to 512 neighbouring positions
- step_count: int32 [1], replicated, may hold values from 2 to 8
- qkv_weight: float32 [3, 768, 768], P(None, None, 'mp'), may hold values from -0.21875 to 0.21875
- qkv_first: float32 [3, 768, 768], P(None, 'dp', 'mp'), may hold values from -0.00061035156 to 0.00061035156
- qkv_second: float32 [3, 768, 768], P(None, 'dp', 'mp'), may hold values from 7.4315953e-09 to 2.9669868e-08
- out_weight: float32 [768, 768], P('mp'), may hold values from -1.75 to 1.75
- out_first: float32 [768, 768], P('mp', 'dp'), may hold values from -0.00061035156 to 0.00061035156
- out_second: float32 [768, 768], P('mp', 'dp'), may hold values from 7.4315953e-09 to 2.9669868e-08
- up_weight: float32 [768, 3072], P(None, 'mp'), may hold values from -0.21875 to 0.21875
- up_first: float32 [768, 3072], P('dp', 'mp'), may hold values from -0.00061035156 to 0.00061035156
- up_second: float32 [768, 3072], P('dp', 'mp'), may hold values from 7.4315953e-09 to 2.9669868e-08
- down_weight: float32 [3072, 768], P('mp'), may hold values from -0.109375 to 0.109375
- down_first: float32 [3072, 768], P('mp', 'dp'), may hold values from -0.00061035156 to 0.00061035156
- down_second: float32 [3072, 768], P('mp', 'dp'), may hold values from 7.4315953e-09 to 2.9669868e-08
- head_params: float32 [5, 12, 64], P(None, 'mp'), may hold values from -2 to 2, as said below
- head_first: float32 [5, 12, 64], P(None, 'mp'), may hold values from -0.00061035156 to 0.00061035156
- head_second: float32 [5, 12, 64], P(None, 'mp'), may hold values from 7.4315953e-09 to 2.9669868e-08
- up_bias: float32 [3072], P('mp'), may hold values from -2 to 2
- upb_first: float32 [3072], P('mp'), may hold values from -0.00061035156 to 0.00061035156
- upb_second: float32 [3072], P('mp'), may hold values from 7.4315953e-09 to 2.9669868e-08
- vec_params: float32 [6, 768], replicated, may hold values from -2 to 2, as said below
- vec_first: float32 [6, 768], replicated, may hold values from -0.00061035156 to 0.00061035156
- vec_second: float32 [6, 768], replicated, may hold values from 7.4315953e-09 to 2.9669868e-08
Outputs:
- block_out: bfloat16 [8, 2048, 768], P('dp')
- grad_input: bfloat16 [8, 2048, 768], P('dp')
- new_qkv: float32 [3, 768, 768], P(None, 'dp', 'mp')
- new_qkv_first: float32 [3, 768, 768], P(None, 'dp', 'mp')
- new_qkv_second: float32 [3, 768, 768], P(None, 'dp', 'mp')
- new_out: float32 [768, 768], P('mp', 'dp')
- new_out_first: float32 [768, 768], P('mp', 'dp')
- new_out_second: float32 [768, 768], P('mp', 'dp')
- new_up: float32 [768, 3072], P('dp', 'mp')
- new_up_first: float32 [768, 3072], P('dp', 'mp')
- new_up_second: float32 [768, 3072], P('dp', 'mp')
- new_down: float32 [3072, 768], P('mp', 'dp')
- new_down_first: float32 [3072, 768], P('mp', 'dp')
- new_down_second: float32 [3072, 768], P('mp', 'dp')
- new_head: float32 [5, 12, 64], P(None, 'mp')
- new_head_first: float32 [5, 12, 64], P(None, 'mp')
- new_head_second: float32 [5, 12, 64], P(None, 'mp')
- new_upb: float32 [3072], P('mp')
- new_upb_first: float32 [3072], P('mp')
- new_upb_second: float32 [3072], P('mp')
- new_vec: float32 [6, 768], replicated
- new_vec_first: float32 [6, 768], replicated
- new_vec_second: float32 [6, 768], replicated
- grad_norm: float32 [1], replicated
- rms_stats: float32 [2], replicated
Inputs may be any that keep to these rules, and one draw needn't show every extreme that they name: `keep_mask`: per sequence each patch is kept with a chance from one half to all; the chance rises with the sequence index. `segment_ids`: within a row ids never fall; each image covers 1 to 512 consecutive slots, one exactly that many. `head_params`: rows 0 to 2 are biases, rows 3 and 4 gains. `vec_params`: rows 0 and 2 are gains, the others biases.
All inputs are finite; a program needn't handle non-finite values.
Results may differ from a plain program's by a relative error of at most 0.012.
Values sent between devices are 32-bit elements; how exact they have to be, the bound alone decides.
No kernel may reach another device: no remote copies, remote signals or barrier semaphores. Data moves between devices by JAX's collectives and lax.ppermute only.
A program may use at most 256 MiB of HBM per device.

v0:
```python
import functools

import jax
import jax.numpy as jnp
from jax import lax
from jax.experimental import pallas as pl
from jax.experimental.pallas import tpu as pltpu
from jax.sharding import PartitionSpec as P

NORM_EPS = 1e-06
CLIP_LIMIT = 1.0
LEARN_RATE = 0.1
BETA_ONE = 0.9
BETA_TWO = 0.95
ADAM_EPS = 1e-08
WEIGHT_DECAY = 0.1
SEG_BOUND = 512
BLOCK = 256
LANES = 128
F32 = jnp.float32
BF16 = jnp.bfloat16


def adam_step(weight, grad, first, second, factor, corr_one, corr_two, decay):
    grad = factor * grad
    first = BETA_ONE * first + (1.0 - BETA_ONE) * grad
    second = BETA_TWO * second + (1.0 - BETA_TWO) * grad * grad
    update = first / corr_one / (jnp.sqrt(second / corr_two) + ADAM_EPS)
    return (weight - LEARN_RATE * (update + decay * weight), first, second)


def dot(left, right, left_dim, right_dim):
    return lax.dot_general(
        left, right, (((left_dim,), (right_dim,)), ((), ())), preferred_element_type=F32
    )


class Links:
    def __init__(self):
        self.dp_size = lax.axis_size("dp")
        self.mp_size = lax.axis_size("mp")
        self.bits = self.dp_size.bit_length() - 1
        self.dp = lax.axis_index("dp")
        self.mp = lax.axis_index("mp")

    def core(self, array):
        return lax.ppermute(array, "mp", [(i, i ^ 1) for i in range(self.mp_size)])

    def half(self, array):
        return lax.ppermute(array, "mp", [(i, i ^ 2) for i in range(self.mp_size)])

    def data(self, array, bit):
        return lax.ppermute(array, "dp", [(i, i ^ (1 << bit)) for i in range(self.dp_size)])

    def bit(self, bit):
        return (self.dp >> bit) & 1

    def sum_all(self, array):
        array = array + self.core(array)
        array = array + self.half(array)
        return self.sum_data(array)

    def sum_data(self, array):
        for bit in range(self.bits):
            array = array + self.data(array, bit)
        return array


def hold(value, *after):
    return lax.optimization_barrier((value, *after))[0]


def quarter_of(links, weight, axis):
    rows = weight.shape[axis] // 4
    return lax.dynamic_slice_in_dim(weight, (links.dp & 3) * rows, rows, axis)


def quarter_spots(links):
    return jnp.stack([(links.dp & 3) ^ change for change in range(4)])


class Reduction:
    def __init__(self, links, grad):
        self.links = links
        self.left = list(range(links.bits - 1, -1, -1))
        self.array = grad.reshape((2,) * links.bits + (grad.shape[0] >> links.bits, grad.shape[1]))

    def send(self, step):
        if step == "half":
            own = self.array.shape[-1] // 2
            self.kept = self.array[..., :own]
            return self.array[..., own:]
        axis = self.left.index(step)
        self.left.remove(step)
        mine = self.links.bit(step)
        self.kept = lax.dynamic_index_in_dim(self.array, mine, axis, keepdims=False)
        return lax.dynamic_index_in_dim(self.array, 1 - mine, axis, keepdims=False)

    def take(self, arrived):
        self.array = self.kept + arrived

    def step(self, step, *after):
        sent = self.send(step)
        sent = hold(sent, *after) if after else sent
        self.take(self.links.half(sent) if step == "half" else self.links.data(sent, step))


def vmem_specs(count):
    return [pl.BlockSpec(memory_space=pltpu.VMEM)] * count


def smem_specs(count):
    return [pl.BlockSpec(memory_space=pltpu.SMEM)] * count


def cost(flops, bytes_accessed, transcendentals=0):
    return pl.CostEstimate(
        flops=int(flops), bytes_accessed=int(bytes_accessed), transcendentals=int(transcendentals)
    )


def normed(values, axis):
    scale = 1.0 / values.shape[axis]
    center = values - jnp.sum(values, axis=axis, keepdims=True) * scale
    spread = jnp.sum(center * center, axis=axis, keepdims=True) * scale
    factor = lax.rsqrt(spread + NORM_EPS)
    return center * factor, factor


def normed_back(grad_hat, hat, factor, axis):
    scale = 1.0 / hat.shape[axis]
    mean = jnp.sum(grad_hat, axis=axis, keepdims=True) * scale
    along = jnp.sum(grad_hat * hat, axis=axis, keepdims=True) * scale
    return factor * (grad_hat - mean - hat * along)


def fold_rows(values):
    return jnp.sum(values.reshape(values.shape[0] // 8, 8, values.shape[1]), axis=0)


def fold_lanes(values):
    total = values[:, :LANES]
    for start in range(LANES, values.shape[1], LANES):
        total = total + values[:, start : start + LANES]
    return total


def column(row, count):
    return jnp.transpose(jnp.broadcast_to(row, (count, row.shape[1])))


def plan_kernel(window, half_ref, seg_ref, keep_ref, plan_ref, qseg_ref, kcode_ref, kept_ref):
    seq_len = seg_ref.shape[1]
    seg = seg_ref[...]
    half = half_ref[0]
    places = lax.broadcasted_iota(jnp.int32, (1, seq_len), 1)
    starts = (seg != pltpu.roll(seg, 1, 1)) & (places > 0)
    ranking = jnp.where(starts, jnp.abs(places - seq_len // 2) * (4 * seq_len) + places, 1 << 30)
    parting = lax.rem(jnp.min(ranking), 4 * seq_len)
    start = pl.multiple_of(half * (seq_len - window), LANES)
    low_valid = jnp.where(half == 0, 0, parting - start)
    high_valid = jnp.where(half == 0, parting, window)
    seg_win = seg_ref[:, pl.ds(start, window)]
    keep_win = keep_ref[:, pl.ds(start, window)]
    spots = lax.broadcasted_iota(jnp.int32, (1, window), 1)
    valid = (spots >= low_valid) & (spots < high_valid)
    qseg_ref[...] = jnp.broadcast_to(seg_win, (8, window))
    kcode_ref[...] = column(jnp.where(keep_win == 1, seg_win, -1), LANES)
    kept_ref[...] = column(jnp.where(valid & (keep_win == 1), 1.0, 0.0), LANES)
    segs = jnp.broadcast_to(seg_win, (8, window))
    lanes = lax.broadcasted_iota(jnp.int32, (8, window), 1)
    block = lax.broadcasted_iota(jnp.int32, (8, window), 0) * BLOCK

    def total(values):
        return jnp.sum(values, axis=1, keepdims=True)

    first_seg = total(jnp.where(lanes == block, segs, 0))
    last_seg = total(jnp.where(lanes == block + (BLOCK - 1), segs, 0))
    low = total(jnp.where(segs < first_seg, 1, 0))
    high = total(jnp.where(segs <= last_seg, 1, 0))
    block_first = block[:, :1]
    low = jnp.maximum(low, low_valid)
    high = jnp.minimum(high, high_valid) + (BLOCK - 1)
    shift = BLOCK.bit_length() - 1
    low, high = low >> shift, high >> shift
    live = (block_first < high_valid) & (block_first + BLOCK > low_valid)
    high = jnp.where(live, high, low)
    lane = lax.broadcasted_iota(jnp.int32, (8, LANES), 1)
    plan = jnp.where(lane == 0, low, jnp.where(lane == 1, high, parting))
    plan_ref[...] = plan


def make_plan(links, seg_row, keep_row, window):
    half = jnp.full((1,), links.mp // 2, jnp.int32)
    return pl.pallas_call(
        functools.partial(plan_kernel, window),
        out_shape=(
            jax.ShapeDtypeStruct((8, LANES), jnp.int32),
            jax.ShapeDtypeStruct((8, window), jnp.int32),
            jax.ShapeDtypeStruct((window, LANES), jnp.int32),
            jax.ShapeDtypeStruct((window, LANES), F32),
        ),
        in_specs=smem_specs(1) + vmem_specs(2),
        out_specs=tuple(vmem_specs(4)),
        compiler_params=pltpu.CompilerParams(vmem_limit_bytes=6 << 20),
        cost_estimate=cost(0, window * 1100),
        name="plan_window",
    )(half, seg_row, keep_row)


def allowed_block(kcode_ref, qseg_ref, key_start, query_start):
    codes = kcode_ref[pl.ds(key_start, BLOCK), :]
    codes = jnp.concatenate([codes] * (BLOCK // LANES), axis=1)
    segs = qseg_ref[0:1, pl.ds(query_start, BLOCK)]
    rows = lax.broadcasted_iota(jnp.int32, (BLOCK, BLOCK), 0)
    cols = lax.broadcasted_iota(jnp.int32, (BLOCK, BLOCK), 1)
    return (codes == segs) | (rows - cols == query_start - key_start)


def project_heads(heads, dim, weight, a_ref, params_ref, qkv_refs, hat_refs, factor_ref):
    tokens = a_ref.shape[0]
    group = heads * dim

    def block(tb, carry):
        ts = pl.multiple_of(tb * BLOCK, BLOCK)
        here = pl.ds(ts, BLOCK)
        rows = a_ref[here, :]
        for which in range(3):
            raw = dot(weight[which][...], rows, 1, 1) + params_ref[:, which : which + 1]
            if which == 2:
                qkv_refs[2][:, here] = raw.astype(BF16)
                continue
            hat, factor = normed(raw.reshape(heads, dim, BLOCK), 1)
            hat = hat.reshape(group, BLOCK)
            gained = hat * params_ref[:, 3 + which : 4 + which]
            if which == 0:
                gained = gained * dim ** (-0.5)
            qkv_refs[which][:, here] = gained.astype(BF16)
            hat_refs[which][:, here] = hat.astype(BF16)
            for head in range(heads):
                spot = (which * heads + head) * 8
                factor_ref[pl.ds(spot, 8), here] = jnp.broadcast_to(factor[head], (8, BLOCK))
        return carry

    lax.fori_loop(0, tokens // BLOCK, block, 0)


def attend(heads, dim, plan_ref, q_ref, k_ref, v_ref, kcode_ref, qseg_ref, o_ref, inv_ref, acc, tot):
    tokens = q_ref.shape[1]

    def query_block(qb, carry):
        qs = pl.multiple_of(qb * BLOCK, BLOCK)
        acc[...] = jnp.zeros_like(acc)
        tot[...] = jnp.zeros_like(tot)

        def key_block(kb, carry):
            ks = pl.multiple_of(kb * BLOCK, BLOCK)
            allowed = allowed_block(kcode_ref, qseg_ref, ks, qs)
            lines = [pl.ds(head * dim, dim) for head in range(heads)]
            scores = [dot(k_ref[rows, pl.ds(ks, BLOCK)], q_ref[rows, pl.ds(qs, BLOCK)], 0, 0) for rows in lines]
            expos = [jnp.where(allowed, jnp.exp(score), 0.0) for score in scores]
            more = [dot(v_ref[rows, pl.ds(ks, BLOCK)], expo.astype(BF16), 1, 0) for rows, expo in zip(lines, expos)]
            for head, rows in enumerate(lines):
                tot[pl.ds(head * 8, 8), :] += fold_rows(expos[head])
                acc[rows, :] += more[head]
            return carry

        lax.fori_loop(plan_ref[qb, 0], plan_ref[qb, 1], key_block, 0)
        for head in range(heads):
            rows = pl.ds(head * dim, dim)
            total = jnp.sum(tot[pl.ds(head * 8, 8), :], axis=0, keepdims=True)
            inverse = jnp.where(total > 0.0, 1.0 / total, 0.0)
            o_ref[rows, pl.ds(qs, BLOCK)] = (acc[rows, :] * inverse).astype(BF16)
            inv_ref[pl.ds(head * 8, 8), pl.ds(qs, BLOCK)] = jnp.broadcast_to(inverse, (8, BLOCK))
        return carry

    lax.fori_loop(0, tokens // BLOCK, query_block, 0)


def own_heads_kernel(
    heads, dim, x_ref, vec_ref, weight_ref, params_ref,
    a_ref, q_ref, k_ref, v_ref, qh_ref, kh_ref, factor_ref, weight,
):
    weight[...] = weight_ref[...].astype(BF16)
    tokens = x_ref.shape[0]

    def norm_block(tb, carry):
        here = pl.ds(pl.multiple_of(tb * BLOCK, BLOCK), BLOCK)
        hat, _ = normed(x_ref[here, :].astype(F32), 1)
        a_ref[here, :] = (hat * vec_ref[0:1, :] + vec_ref[1:2, :]).astype(BF16)
        return carry

    lax.fori_loop(0, tokens // BLOCK, norm_block, 0)
    project_heads(
        heads, dim, [weight.at[k] for k in range(3)], a_ref, params_ref, (q_ref, k_ref, v_ref),
        (qh_ref, kh_ref), factor_ref,
    )


def other_heads_kernel(
    heads, dim, spots_ref, a_ref, own_ref, p0, p1, p2, p3, params_ref,
    q_ref, k_ref, v_ref, qh_ref, kh_ref, factor_ref, qk_ref, value_ref,
):
    group = heads * dim
    places = [
        (qk_ref.at[pl.ds(0, group)], qk_ref.at[pl.ds(2 * group, group)]),
        (qk_ref.at[pl.ds(group, group)], qk_ref.at[pl.ds(3 * group, group)]),
        (value_ref.at[pl.ds(0, group)], value_ref.at[pl.ds(group, group)]),
    ]
    for which, (own_place, place) in enumerate(places):
        own_place[...] = own_ref[which].astype(BF16)
        for index, piece in enumerate((p0, p1, p2, p3)):
            count = piece.shape[1]
            spot = pl.multiple_of(spots_ref[index] * count, 16)
            place[pl.ds(spot, count), :] = piece[which].astype(BF16)
    project_heads(
        heads, dim, [place for _, place in places], a_ref, params_ref, (q_ref, k_ref, v_ref), (qh_ref, kh_ref), factor_ref
    )


def attention_kernel(
    heads, dim, plan_ref, q_ref, k_ref, v_ref, kcode_ref, qseg_ref, o_ref, inv_ref, acc, tot
):
    attend(heads, dim, plan_ref, q_ref, k_ref, v_ref, kcode_ref, qseg_ref, o_ref, inv_ref, acc, tot)


def out_kernel(o_own_ref, o_other_ref, own_ref, other_ref, part_ref, weight, o_cat):
    group = own_ref.shape[0]

    @pl.when(pl.program_id(0) == 0)
    def _():
        weight[pl.ds(0, group), :] = own_ref[...].astype(BF16)
        weight[pl.ds(group, group), :] = other_ref[...].astype(BF16)

    o_cat[pl.ds(0, group), :] = o_own_ref[...]
    o_cat[pl.ds(group, group), :] = o_other_ref[...]
    part_ref[...] = dot(o_cat[...], weight[...], 0, 0)


def head_shapes(group, heads, tokens):
    narrow = jax.ShapeDtypeStruct((group, tokens), BF16)
    return [*(narrow,) * 5, jax.ShapeDtypeStruct((heads * 16, tokens), F32)]


def o_shapes(group, heads, tokens):
    return [
        jax.ShapeDtypeStruct((group, tokens), BF16),
        jax.ShapeDtypeStruct((heads * 8, tokens), F32),
    ]


def own_heads(x_win, vec_params, weight, params, heads, dim):
    tokens, width = x_win.shape
    group = heads * dim
    return pl.pallas_call(
        functools.partial(own_heads_kernel, heads, dim),
        out_shape=[
            jax.ShapeDtypeStruct((tokens, width), BF16),
            *head_shapes(group, heads, tokens),
        ],
        in_specs=vmem_specs(4),
        out_specs=vmem_specs(7),
        scratch_shapes=[pltpu.VMEM((3, group, width), BF16)],
        cost_estimate=cost(tokens * width * group * 6, tokens * width * 8),
        name="heads_own",
    )(x_win, vec_params, weight, params)


def other_heads(spots, a_first, own_weight, pieces, params, heads, dim):
    tokens, width = a_first.shape
    group = heads * dim
    return pl.pallas_call(
        functools.partial(other_heads_kernel, heads, dim),
        out_shape=[
            *head_shapes(group, heads, tokens),
            jax.ShapeDtypeStruct((4 * group, width), BF16),
            jax.ShapeDtypeStruct((2 * group, width), BF16),
        ],
        in_specs=smem_specs(1) + vmem_specs(7),
        out_specs=vmem_specs(8),
        cost_estimate=cost(tokens * width * group * 6, tokens * width * 8),
        name="heads_other",
    )(spots, a_first, own_weight, *pieces, params)


def attention(plan, query, key, value, kcode, qseg, heads, dim):
    group, tokens = query.shape
    pairs = heads * tokens * 3 * BLOCK
    return pl.pallas_call(
        functools.partial(attention_kernel, heads, dim),
        out_shape=o_shapes(group, heads, tokens),
        in_specs=smem_specs(1) + vmem_specs(5),
        out_specs=vmem_specs(2),
        scratch_shapes=[pltpu.VMEM((group, BLOCK), F32), pltpu.VMEM((heads * 8, BLOCK), F32)],
        cost_estimate=cost(pairs * dim * 4, group * tokens * 8, pairs),
        name="attention",
    )(plan, query, key, value, kcode, qseg)


def out_project(o_own, o_other, out_own, out_other):
    group, tokens = o_own.shape
    width = out_own.shape[1]
    cols = pl.BlockSpec((group, BLOCK), lambda i: (0, i))
    return pl.pallas_call(
        out_kernel,
        grid=(tokens // BLOCK,),
        out_shape=jax.ShapeDtypeStruct((tokens, width), F32),
        in_specs=[cols, cols, whole_spec(out_own.shape), whole_spec(out_other.shape)],
        out_specs=rows_spec(width),
        scratch_shapes=[
            pltpu.VMEM((2 * group, width), BF16),
            pltpu.VMEM((2 * group, BLOCK), BF16),
        ],
        compiler_params=pltpu.CompilerParams(vmem_limit_bytes=12 << 20),
        cost_estimate=cost(tokens * width * group * 4, tokens * width * 6),
        name="out_project",
    )(o_own, o_other, out_own, out_other)


def attention_back_kernel(
    heads, dim, plan_ref, q_ref, k_ref, v_ref, qh_ref, kh_ref, factor_ref, o_ref, inv_ref, do_ref,
    params_ref, kcode_ref, qseg_ref, *rest,
):
    draw_qk_ref, draw_v_ref = rest[-7:-5]
    out_sums_ref, dq_ref, dk_ref, dv_ref, sums_ref = rest[-5:]
    group, tokens = q_ref.shape
    for ref in (dq_ref, dk_ref, dv_ref, sums_ref):
        ref[...] = jnp.zeros_like(ref)

    def query_block(qb, carry):
        qs = pl.multiple_of(qb * BLOCK, BLOCK)
        here = pl.ds(qs, BLOCK)
        deltas = []
        inverses = []
        for head in range(heads):
            rows = pl.ds(head * dim, dim)
            products = do_ref[rows, here].astype(F32) * o_ref[rows, here].astype(F32)
            deltas.append(jnp.sum(products, axis=0, keepdims=True))
            inverses.append(inv_ref[pl.ds(head * 8, 1), here])

        def key_block(kb, carry):
            ks = pl.multiple_of(kb * BLOCK, BLOCK)
            there = pl.ds(ks, BLOCK)
            allowed = allowed_block(kcode_ref, qseg_ref, ks, qs)
            lines = [pl.ds(head * dim, dim) for head in range(heads)]
            keys = [k_ref[rows, there] for rows in lines]
            queries = [q_ref[rows, here] for rows in lines]
            grads = [do_ref[rows, here] for rows in lines]
            scores = [dot(key, query, 0, 0) for key, query in zip(keys, queries)]
            grad_probs = [dot(v_ref[rows, there], grad, 0, 0) for rows, grad in zip(lines, grads)]
            added = []
            for head in range(heads):
                probs = jnp.where(allowed, jnp.exp(scores[head]), 0.0) * inverses[head]
                grad_scores = (probs * (grad_probs[head] - deltas[head])).astype(BF16)
                added.append((
                    dot(grads[head], probs.astype(BF16), 1, 1),
                    dot(queries[head], grad_scores, 1, 1),
                    dot(keys[head], grad_scores, 1, 0),
                ))
            for rows, (more_v, more_k, more_q) in zip(lines, added):
                dv_ref[rows, there] += more_v
                dk_ref[rows, there] += more_k
                dq_ref[rows, here] += more_q
            return carry

        lax.fori_loop(plan_ref[qb, 0], plan_ref[qb, 1], key_block, 0)
        return carry

    lax.fori_loop(0, tokens // BLOCK, query_block, 0)

    def token_block(tb, carry):
        here = pl.ds(pl.multiple_of(tb * BLOCK, BLOCK), BLOCK)
        for which, (grad_ref, hat_ref) in enumerate(((dq_ref, qh_ref), (dk_ref, kh_ref), (dv_ref, None))):
            rows = pl.ds(which * group, group)
            grad = grad_ref[:, here]
            if hat_ref is not None:
                if which == 0:
                    grad = grad * dim ** (-0.5)
                hat = hat_ref[:, here].astype(F32)
                sums_ref[pl.ds((3 + which) * group, group), :] += fold_lanes(grad * hat)
                grad = grad * params_ref[:, 3 + which : 4 + which]
                parts = []
                for head in range(heads):
                    lines = slice(head * dim, (head + 1) * dim)
                    factor = factor_ref[pl.ds((which * heads + head) * 8, 1), here]
                    parts.append(normed_back(grad[lines], hat[lines], factor, 0))
                grad = jnp.concatenate(parts, axis=0)
            rounded = grad.astype(BF16)
            if which < 2:
                draw_qk_ref[rows, here] = rounded
            else:
                draw_v_ref[:, here] = rounded
            sums_ref[rows, :] += fold_lanes(rounded.astype(F32))
        return carry

    lax.fori_loop(0, tokens // BLOCK, token_block, 0)
    out_sums_ref[...] = jnp.sum(jnp.transpose(sums_ref[...]), axis=0, keepdims=True)


def attention_back(plan, saved, grad_o, params, kcode, qseg, heads, dim, draws=None):
    group, tokens = saved[0].shape
    pairs = heads * tokens * 3 * BLOCK
    which = 0 if draws is None else 1
    sums = -(-5 * group // LANES) * LANES
    inputs = [*saved, grad_o, params, kcode, qseg]
    in_specs = smem_specs(1) + [whole_spec(x.shape) for x in inputs]
    aliases = {}
    if draws is not None:
        aliases = {1 + len(inputs) + k: k for k in range(2)}
        inputs += draws
        in_specs += [pl.BlockSpec(memory_space=pl.ANY)] * 2
    return pl.pallas_call(
        functools.partial(attention_back_kernel, heads, dim),
        grid=(1,),
        out_shape=[
            jax.ShapeDtypeStruct((4 * group, tokens), BF16),
            jax.ShapeDtypeStruct((2 * group, tokens), BF16),
            jax.ShapeDtypeStruct((1, sums), F32),
        ],
        in_specs=in_specs,
        out_specs=[
            pl.BlockSpec((2 * group, tokens), lambda i: (which, 0)),
            pl.BlockSpec((group, tokens), lambda i: (which, 0)),
            whole_spec((1, sums)),
        ],
        scratch_shapes=[
            *(pltpu.VMEM((group, tokens), F32),) * 3,
            pltpu.VMEM((sums, LANES), F32),
        ],
        input_output_aliases=aliases,
        compiler_params=pltpu.CompilerParams(vmem_limit_bytes=16 << 20),
        cost_estimate=cost(pairs * dim * 10, group * tokens * 30, pairs),
        name="attention_back",
    )(plan, *inputs)


ERFC_TERMS = (
    0.16918800576031592, 0.17071521752915575, 0.14833923939584578, 0.2149257797248009,
    -0.09465005158893602, 0.5477190245253036, -0.5122771874066157, 0.4855627631921905,
    -0.1295228107166713,
)


def gelu_and_slope(values):
    t = 1.0 / (1.0 + (0.3 * 0.5**0.5) * jnp.abs(values))
    poly = ERFC_TERMS[-1]
    for term in ERFC_TERMS[-2::-1]:
        poly = poly * t + term
    bell = jnp.exp(values * values * -0.5)
    low_tail = 0.5 * (t * poly) * bell
    below = jnp.where(values > 0.0, 1.0 - low_tail, low_tail)
    return values * below, below + values * bell * 0.3989422804014327


def mlp_half(a, dmlp, up, down, bias):
    upper = dot(a, up, 1, 0) + bias
    gated, slope = gelu_and_slope(upper)
    gated = gated.astype(BF16)
    grad_gated = dot(dmlp, down, 1, 1)
    grad_upper = (grad_gated * slope).astype(BF16)
    return gated, grad_upper, dot(gated, down, 1, 0), dot(grad_upper, up, 1, 1)


def own_mlp_kernel(
    x_ref, mine_ref, peer_ref, cot_ref, kept_ref, vec_ref, up_ref, down_ref, bias_ref,
    hidden_ref, a_ref, dmlp_ref, g_ref, du_ref, mlp_ref, da_ref, bias_out, attn_out, up, down, bias_sums, attn_sums,
):
    @pl.when(pl.program_id(0) == 0)
    def _():
        up[...] = up_ref[...].astype(BF16)
        down[...] = down_ref[...].astype(BF16)
        bias_sums[...] = jnp.zeros_like(bias_sums)
        attn_sums[...] = jnp.zeros_like(attn_sums)

    kept = kept_ref[:, 0:1]
    attn = mine_ref[...] + peer_ref[...] + vec_ref[4:5, :]
    attn_sums[...] += fold_rows(kept * attn * attn)
    hidden = x_ref[...].astype(F32) + attn
    hidden_ref[...] = hidden
    hat, _ = normed(hidden, 1)
    a = (hat * vec_ref[2:3, :] + vec_ref[3:4, :]).astype(BF16)
    a_ref[...] = a
    dmlp = (cot_ref[...].astype(F32) * kept).astype(BF16)
    dmlp_ref[...] = dmlp
    gated, grad_upper, mlp, da = mlp_half(a, dmlp, up[...], down[...], bias_ref[...])
    g_ref[...] = gated
    du_ref[...] = grad_upper
    mlp_ref[...] = mlp
    da_ref[...] = da
    bias_sums[...] += fold_rows(grad_upper.astype(F32))

    @pl.when(pl.program_id(0) == pl.num_programs(0) - 1)
    def _():
        bias_out[...] = jnp.sum(bias_sums[...], axis=0, keepdims=True)
        attn_out[...] = jnp.sum(attn_sums[...], axis=0, keepdims=True)


def other_mlp_kernel(
    spots_ref, a_ref, dmlp_ref, mlp_in_ref, da_in_ref, base, near_a, near_b, far_a, far_b, bias_ref,
    g_ref, du_ref, mlp_ref, da_left_ref, da_right_ref, bias_out, up, down, bias_sums,
):
    @pl.when(pl.program_id(0) == 0)
    def _():
        count = near_a.shape[1]
        for change, first, second in (
            (0, base.at[:, pl.ds(0, count)], base.at[:, pl.ds(count, count)]),
            (1, near_a, far_b.at[0]),
            (2, far_a.at[0], near_b),
            (3, far_a.at[1], far_b.at[1]),
        ):
            for which, piece in enumerate((first, second)):
                spot = pl.multiple_of((spots_ref[change] * 2 + which) * count, 16)
                up[pl.ds(spot, count), :] = piece[0].astype(BF16)
                down[pl.ds(spot, count), :] = piece[1].astype(BF16)
        bias_sums[...] = jnp.zeros_like(bias_sums)

    gated, grad_upper, mlp, da = mlp_half(
        a_ref[...], dmlp_ref[...], up[...], down[...], bias_ref[...]
    )
    g_ref[...] = gated
    du_ref[...] = grad_upper
    mlp_ref[...] = mlp_in_ref[...] + mlp
    da = da_in_ref[...] + da
    cut = da_left_ref.shape[1]
    da_left_ref[...], da_right_ref[...] = da[:, :cut], da[:, cut:]
    bias_sums[...] += fold_rows(grad_upper.astype(F32))

    @pl.when(pl.program_id(0) == pl.num_programs(0) - 1)
    def _():
        bias_out[...] = jnp.sum(bias_sums[...], axis=0, keepdims=True)


def rows_spec(width):
    return pl.BlockSpec((BLOCK, width), lambda i: (i, 0))


def whole_spec(shape):
    return pl.BlockSpec(shape, lambda *_: (0,) * len(shape), pipeline_mode=pl.Buffered(1))


def sums_spec(rows, width):
    return pl.BlockSpec((rows, width), lambda *_: (0, 0))


def own_mlp(x_win, mine, peer, cot, kept, vec_params, up_weight, down_weight, bias):
    tokens, width = x_win.shape
    units = up_weight.shape[1]
    wide = rows_spec(width)
    struct = jax.ShapeDtypeStruct
    return pl.pallas_call(
        own_mlp_kernel,
        grid=(tokens // BLOCK,),
        out_shape=[
            struct((tokens, width), F32),
            struct((tokens, width), BF16),
            struct((tokens, width), BF16),
            struct((tokens, units), BF16),
            struct((tokens, units), BF16),
            struct((tokens, width), F32),
            struct((tokens, width), F32),
            struct((1, units), F32),
            struct((1, width), F32),
        ],
        in_specs=[
            wide, wide, wide, wide, rows_spec(LANES), whole_spec(vec_params.shape),
            whole_spec(up_weight.shape), whole_spec(down_weight.shape), whole_spec(bias.shape),
        ],
        out_specs=[
            wide, wide, wide, rows_spec(units), rows_spec(units), wide, wide,
            sums_spec(1, units), sums_spec(1, width),
        ],
        scratch_shapes=[
            pltpu.VMEM(up_weight.shape, BF16),
            pltpu.VMEM(down_weight.shape, BF16),
            pltpu.VMEM((8, units), F32),
            pltpu.VMEM((8, width), F32),
        ],
        cost_estimate=cost(8 * tokens * width * units, tokens * width * 40, tokens * units * 2),
        name="mlp_own",
    )(x_win, mine, peer, cot, kept, vec_params, up_weight, down_weight, bias)


def other_mlp(spots, a_second, dmlp, mlp_part, da_part, pieces, bias):
    tokens, width = a_second.shape
    units = bias.shape[1]
    wide = rows_spec(width)
    struct = jax.ShapeDtypeStruct
    return pl.pallas_call(
        other_mlp_kernel,
        grid=(tokens // BLOCK,),
        out_shape=[
            struct((tokens, units), BF16),
            struct((tokens, units), BF16),
            struct((tokens, width), F32),
            struct((tokens, width // 2), F32),
            struct((tokens, width // 2), F32),
            struct((1, units), F32),
        ],
        in_specs=[
            *smem_specs(1), wide, wide, wide, wide,
            *(whole_spec(piece.shape) for piece in pieces), whole_spec(bias.shape),
        ],
        out_specs=[
            rows_spec(units), rows_spec(units), wide, *(rows_spec(width // 2),) * 2, sums_spec(1, units),
        ],
        input_output_aliases={3: 2},
        scratch_shapes=[
            pltpu.VMEM((width, units), BF16),
            pltpu.VMEM((units, width), BF16),
            pltpu.VMEM((8, units), F32),
        ],
        cost_estimate=cost(8 * tokens * width * units, tokens * width * 28, tokens * units * 2),
        name="mlp_other",
    )(spots, a_second, dmlp, mlp_part, da_part, *pieces, bias)


def hidden_back_kernel(
    group, hidden_ref, mine_left, mine_right, peer_left, peer_right, cot_ref, kept_ref, vec_ref, out_own_ref, out_other_ref,
    dh_ref, dattn_ref, do_own_ref, do_other_ref, sums_out, out_weight, sums_ref,
):
    @pl.when(pl.program_id(0) == 0)
    def _():
        out_weight[pl.ds(0, group), :] = out_own_ref[...].astype(BF16)
        out_weight[pl.ds(group, group), :] = out_other_ref[...].astype(BF16)
        sums_ref[...] = jnp.zeros_like(sums_ref)

    hat, factor = normed(hidden_ref[...], 1)
    da = jnp.concatenate(
        [mine_left[...] + peer_left[...], mine_right[...] + peer_right[...]], axis=1
    )
    dy = cot_ref[...].astype(F32) * kept_ref[:, 0:1]
    dh = dy + normed_back(da * vec_ref[2:3, :], hat, factor, 1)
    dh_ref[...] = dh
    dattn = dh.astype(BF16)
    dattn_ref[...] = dattn
    grads = dot(out_weight[...], dattn, 1, 1).astype(BF16)
    do_own_ref[...] = grads[:group]
    do_other_ref[...] = grads[group:]
    sums_ref[0:8, :] += fold_rows(da * hat)
    sums_ref[8:16, :] += fold_rows(da)
    sums_ref[16:24, :] += fold_rows(dattn.astype(F32))
    sums_ref[24:32, :] += fold_rows(dy.astype(BF16).astype(F32))

    @pl.when(pl.program_id(0) == pl.num_programs(0) - 1)
    def _():
        for row in range(4):
            total = jnp.sum(sums_ref[8 * row : 8 * row + 8, :], axis=0, keepdims=True)
            sums_out[row : row + 1, :] = total


def hidden_back(hidden, mine, peer, cot, kept, vec_params, out_own, out_other):
    tokens, width = hidden.shape
    group = out_own.shape[0]
    wide = rows_spec(width)
    cols = pl.BlockSpec((group, BLOCK), lambda i: (0, i))
    struct = jax.ShapeDtypeStruct
    return pl.pallas_call(
        functools.partial(hidden_back_kernel, group),
        grid=(tokens // BLOCK,),
        out_shape=[
            struct((tokens, width), F32),
            struct((tokens, width), BF16),
            struct((group, tokens), BF16),
            struct((group, tokens), BF16),
            struct((4, width), F32),
        ],
        in_specs=[
            wide, *(rows_spec(width // 2),) * 4, wide, rows_spec(LANES), whole_spec(vec_params.shape),
            whole_spec(out_own.shape), whole_spec(out_other.shape),
        ],
        out_specs=[wide, wide, cols, cols, sums_spec(4, width)],
        scratch_shapes=[pltpu.VMEM((2 * group, width), BF16), pltpu.VMEM((32, width), F32)],
        compiler_params=pltpu.CompilerParams(vmem_limit_bytes=22 << 20),
        cost_estimate=cost(4 * tokens * width * group, tokens * width * 22),
        name="hidden_back",
    )(hidden, *mine, *peer, cot, kept, vec_params, out_own, out_other)


def input_back_kernel(
    core_ref, mine_ref, peer_ref, x_ref, dh_ref, vec_ref, left_ref, right_ref, sums_out, sums_ref
):
    @pl.when(pl.program_id(0) == 0)
    def _():
        sums_ref[...] = jnp.zeros_like(sums_ref)

    hat, factor = normed(x_ref[...].astype(F32), 1)
    da = mine_ref[...] + peer_ref[...]
    out = dh_ref[...] + normed_back(da * vec_ref[0:1, :], hat, factor, 1)
    cut = left_ref.shape[1]
    left_ref[...], right_ref[...] = out[:, :cut], out[:, cut:]
    sums_ref[0:8, :] += fold_rows(da * hat)
    sums_ref[8:16, :] += fold_rows(da)

    @pl.when(pl.program_id(0) == pl.num_programs(0) - 1)
    def _():
        for row in range(2):
            total = jnp.sum(sums_ref[8 * row : 8 * row + 8, :], axis=0, keepdims=True)
            sums_out[row : row + 1, :] = total


def input_back(core, mine, peer, x_win, dh, vec_params):
    half_rows, width = peer.shape
    step = LANES
    count = half_rows // step
    near = pl.BlockSpec((step, width), lambda i, core_ref: (i, 0))
    left = pl.BlockSpec((step, width // 2), lambda i, core_ref: (i, 0))
    window = pl.BlockSpec((step, width), lambda i, core_ref: (core_ref[0] * count + i, 0))
    struct = jax.ShapeDtypeStruct
    return pl.pallas_call(
        input_back_kernel,
        grid_spec=pltpu.PrefetchScalarGridSpec(
            num_scalar_prefetch=1,
            grid=(count,),
            in_specs=[window, near, window, window, whole_spec(vec_params.shape)],
            out_specs=[left, left, sums_spec(2, width)],
            scratch_shapes=[pltpu.VMEM((16, width), F32)],
        ),
        out_shape=[
            struct((half_rows, width // 2), F32),
            struct((half_rows, width // 2), F32),
            struct((2, width), F32),
        ],
        cost_estimate=cost(0, half_rows * width * 18),
        name="input_back",
    )(core, mine, peer, x_win, dh, vec_params)


def last_gradients_kernel(
    group, a_ref, dattn_ref, qk_ref, v_ref, o_own_ref, o_other_ref, qk_own_out, qk_other_out, vo_out
):
    a, dattn = a_ref[...], dattn_ref[...]
    query_key = jnp.transpose(dot(qk_ref[...], a, 1, 0))
    qk_own_out[...] = query_key[:, : 2 * group]
    qk_other_out[...] = query_key[:, 2 * group :]
    value = dot(v_ref[...], a, 1, 0)
    own, other = dot(o_own_ref[...], dattn, 1, 0), dot(o_other_ref[...], dattn, 1, 0)
    rows = jnp.concatenate([value[:group], own, value[group:], other], axis=0)
    vo_out[...] = jnp.transpose(rows)


def last_gradients(a_first, dattn, draw_qk, draw_v, o_own, o_other):
    tokens, width = a_first.shape
    group = o_own.shape[0]
    cols = pl.BlockSpec((tokens, BLOCK), lambda i: (0, i))
    narrow, wide = rows_spec(2 * group), rows_spec(4 * group)
    struct = jax.ShapeDtypeStruct
    inputs = (draw_qk, draw_v, o_own, o_other)
    return pl.pallas_call(
        functools.partial(last_gradients_kernel, group),
        grid=(width // BLOCK,),
        out_shape=[
            struct((width, 2 * group), F32),
            struct((width, 2 * group), F32),
            struct((width, 4 * group), F32),
        ],
        in_specs=[cols, cols, *(whole_spec(x.shape) for x in inputs)],
        out_specs=[narrow, narrow, wide],
        compiler_params=pltpu.CompilerParams(vmem_limit_bytes=20 << 20),
        cost_estimate=cost(16 * tokens * width * group, tokens * width * 12),
        name="last_gradients",
    )(a_first, dattn, *inputs)


def pack_kernel(
    core_ref, first_ref, second_ref, kept_ref, attn_ref, mlp_ref,
    own_ref, other_ref, own_bias_ref, other_bias_ref, mine_ref, away_ref,
):
    width = mine_ref.shape[1]
    once = jnp.where(core_ref[0] == 0, 1.0, 0.0)
    count = jnp.sum(kept_ref[...]) * (once / kept_ref.shape[1])
    attn = jnp.sum(attn_ref[...]) * once
    lane = lax.broadcasted_iota(jnp.int32, (1, width), 1)
    stats = jnp.where(lane == 0, count, jnp.where(lane == 1, attn, jnp.where(lane == 2, mlp_ref[0], 0.0)))
    sums, units = own_ref.shape[1], own_bias_ref.shape[1]
    for ref, head, bias in ((mine_ref, own_ref, own_bias_ref), (away_ref, other_ref, other_bias_ref)):
        ref[...] = jnp.zeros_like(ref)
        ref[0:2, :] = first_ref[...]
        ref[2:6, :] = second_ref[...] * once
        ref[6:7, :] = stats
        row = 8
        for source, size in ((head, sums), (bias, units)):
            for start in range(0, size, width):
                length = min(width, size - start)
                ref[row : row + 1, :length] = source[:, start : start + length]
                row += 1


def pack_small(core, first, second, kept, attn, mlp_sq, own, other, own_bias, other_bias):
    width = first.shape[1]
    inputs = (first, second, kept, attn)
    more = (own, other, own_bias, other_bias)
    rows = 8 + -(-own.shape[1] // width) + -(-own_bias.shape[1] // width)
    struct = jax.ShapeDtypeStruct((-(-rows // 8) * 8, width), F32)
    return pl.pallas_call(
        pack_kernel,
        out_shape=[struct, struct],
        in_specs=smem_specs(1) + vmem_specs(4) + smem_specs(1) + vmem_specs(4),
        out_specs=vmem_specs(2),
        compiler_params=pltpu.CompilerParams(vmem_limit_bytes=6 << 20),
        cost_estimate=cost(0, kept.size * 4),
        name="pack_small",
    )(core, *inputs, mlp_sq, *more)


def update_kernel(decays, *refs):
    scalars, count = refs[0], len(decays)
    inputs, outputs = refs[1 : 1 + 4 * count], refs[1 + 4 * count :]
    factor, corr_one, corr_two = scalars[0], scalars[1], scalars[2]
    for index, decay in enumerate(decays):
        weight_ref, grad_ref, first_ref, second_ref = inputs[4 * index : 4 * index + 4]
        shape = weight_ref.shape
        if index == 0:
            size = shape[2]
            spots = [(k, grad_ref[:, k * size : (k + 1) * size]) for k in range(shape[0])]
        elif index == 1:
            spots = [(slice(None), jnp.transpose(grad_ref[:, grad_ref.shape[1] - shape[0] :]))]
        elif index == 2:
            spots = [(slice(None), grad_ref[:, grad_ref.shape[1] - shape[1] :])]
        elif index == 3:
            spots = [(slice(None), grad_ref[:, : shape[1]])]
        else:
            spots = [(slice(None), grad_ref[...])]
        for spot, grad in spots:
            results = adam_step(
                weight_ref[spot], grad, first_ref[spot], second_ref[spot], factor, corr_one, corr_two, decay
            )
            for ref, value in zip(outputs[3 * index : 3 * index + 3], results):
                ref[spot] = value


def update(scalars, groups, decays):
    inputs = [array for group in groups for array in group]
    shapes = [
        jax.ShapeDtypeStruct(group[0].shape, F32) for group in groups for _ in range(3)
    ]
    results = pl.pallas_call(
        functools.partial(update_kernel, decays),
        out_shape=shapes,
        in_specs=smem_specs(1) + vmem_specs(len(inputs)),
        out_specs=vmem_specs(len(shapes)),
        cost_estimate=cost(0, sum(28 * group[0].size for group in groups)),
        name="update",
    )(scalars, *inputs)
    return [results[3 * k : 3 * k + 3] for k in range(len(groups))]


def join_kernel(half_rows, window, pieces, info_ref, factor_ref, shift_ref, *refs):
    out_ref = refs[-1]
    seq_len = out_ref.shape[1]
    core, half, parting = info_ref[0], info_ref[1], info_ref[2]
    factor = factor_ref[0]
    step = LANES
    offset = seq_len - window
    start = 0
    for piece in range(pieces):
        mine_ref, near_ref, far_ref, far_near_ref = refs[4 * piece : 4 * piece + 4]
        cols = slice(start, start + mine_ref.shape[1])
        start += mine_ref.shape[1]
        shift = shift_ref[:, cols]

        def rows_of(which, row, mine=mine_ref, near=near_ref, far=far_ref, far_near=far_near_ref):
            from_core = row // half_rows
            spot = pl.ds(pl.multiple_of(row - from_core * half_rows, step), step)
            same = core == from_core
            return jnp.where(
                half == which,
                jnp.where(same, mine[spot, :], near[spot, :]),
                jnp.where(same, far[spot, :], far_near[spot, :]),
            )

        def store(row, values, cols=cols, shift=shift):
            spot = pl.ds(pl.multiple_of(row, step), step)
            out_ref[0, spot, cols] = (values * factor + shift).astype(BF16)

        def first(block, carry, rows_of=rows_of, store=store):
            store(block * step, rows_of(0, block * step))
            return carry

        def middle(block, carry, rows_of=rows_of, store=store):
            row = block * step
            places = row + lax.broadcasted_iota(jnp.int32, (step, 1), 0)
            store(row, jnp.where(places < parting, rows_of(0, row), rows_of(1, row - offset)))
            return carry

        def second(block, carry, rows_of=rows_of, store=store):
            store(block * step, rows_of(1, block * step - offset))
            return carry

        lax.fori_loop(0, offset // step, first, 0)
        lax.fori_loop(offset // step, window // step, middle, 0)
        lax.fori_loop(window // step, seq_len // step, second, 0)


def join_sequence(links, pieces, parting, seq_len, window, factor, shift):
    half_rows = pieces[0][0].shape[0]
    width = shift.shape[1]
    info = jnp.stack([links.mp % 2, links.mp // 2, parting]).astype(jnp.int32)
    arrays = [array for piece in pieces for array in piece]
    return pl.pallas_call(
        functools.partial(join_kernel, half_rows, window, len(pieces)),
        out_shape=jax.ShapeDtypeStruct((1, seq_len, width), BF16),
        in_specs=smem_specs(2) + vmem_specs(1 + len(arrays)),
        out_specs=pl.BlockSpec(memory_space=pltpu.VMEM),
        cost_estimate=cost(0, half_rows * width * 16 + seq_len * width * 2),
        name="join_sequence",
    )(info, factor, shift, *arrays)


def local(
    patches, cotangent, keep_mask, segment_ids, step_count,
    qkv_weight, qkv_first, qkv_second,
    out_weight, out_first, out_second,
    up_weight, up_first, up_second,
    down_weight, down_first, down_second,
    head_params, head_first, head_second,
    up_bias, upb_first, upb_second,
    vec_params, vec_first, vec_second,
):
    links = Links()
    seq_len, width = patches.shape[1:]
    heads, dim = head_params.shape[1:]
    group = heads * dim
    units = up_weight.shape[1]
    window = seq_len // 2 + SEG_BOUND // 2
    half_rows = window // 2
    core = links.mp % 2
    start = (links.mp // 2) * (seq_len - window)

    qkv_flip = jnp.swapaxes(qkv_weight, 1, 2)
    qkv_base = links.half(quarter_of(links, qkv_flip, 1))
    small = jnp.concatenate([head_params.reshape(-1), up_bias])
    small_other = links.half(small)
    head_other = small_other[: head_params.size].reshape(head_params.shape)

    def columns(params):
        return jnp.pad(params.reshape(params.shape[0], group).T, ((0, 0), (0, 3)))

    head_cols = columns(head_params)
    other_cols = columns(head_other)
    upb_own = up_bias.reshape(1, units)
    upb_other = small_other[head_params.size :].reshape(1, units)

    plan, qseg, kcode, kept = make_plan(links, segment_ids, keep_mask, window)
    parting = plan[0, 2]
    x_win = lax.dynamic_slice_in_dim(patches[0], start, window, 0)
    cot_win = lax.dynamic_slice_in_dim(cotangent[0], start, window, 0)
    a_first, *own = own_heads(x_win, vec_params, qkv_flip, head_cols, heads, dim)

    qkv_base = hold(qkv_base, own[0])
    qkv_pieces = [qkv_base, links.data(qkv_base, 0), links.data(qkv_base, 1)]
    both = [(i, i ^ 3) for i in range(links.dp_size)]
    qkv_pieces.append(lax.ppermute(qkv_base, "dp", both))
    spots = quarter_spots(links)
    up_early, down_early, _, _ = lax.optimization_barrier(
        (up_weight, down_weight, qkv_base, small_other)
    )
    mlp_base = links.half(quarter_of(links, jnp.stack([up_early, down_early]), 1))
    own += attention(plan, hold(own[0], qkv_base), own[1], own[2], kcode, qseg, heads, dim)

    qkv_pieces = list(lax.optimization_barrier((*qkv_pieces, own[6]))[:4])
    *other, qk_cat, value_cat = other_heads(
        spots, hold(a_first, cot_win), qkv_flip, qkv_pieces, other_cols, heads, dim
    )
    mlp_base = hold(mlp_base, other[0])
    out_other = links.half(hold(out_weight, own[6]))
    eighth = mlp_base.shape[1] // 2
    part_a, part_b = mlp_base[:, :eighth], mlp_base[:, eighth:]
    near_a, near_b = links.data(part_a, 0), links.data(part_b, 1)
    other += attention(plan, hold(other[0], mlp_base), other[1], other[2], kcode, qseg, heads, dim)
    o_other, near_a, near_b = lax.optimization_barrier((other[6], near_a, near_b))
    attn_part = out_project(own[6], o_other, out_weight, out_other)
    pair_a, pair_b = jnp.stack([part_a, near_a]), jnp.stack([part_b, near_b])
    far_a, far_b = links.data(pair_a, 1), links.data(pair_b, 0)
    attn_peer = links.core(attn_part)
    hidden, a_second, dmlp, gated, grad_upper, mlp_part, da_part, upb_sums, attn_sums = own_mlp(
        x_win, attn_part, attn_peer, cot_win, kept, vec_params, up_weight, down_weight, upb_own
    )
    down, up = Reduction(links, dot(dmlp, gated, 0, 0)), Reduction(links, dot(a_second, grad_upper, 0, 0))
    down_sent, up_sent = down.send(0), up.send(1)
    down_got, up_got = links.data(down_sent, 0), links.data(up_sent, 1)
    gated, grad_upper, mlp_part, *da_parts, upb_sums_other = other_mlp(
        spots, hold(a_second, down_sent, up_sent), dmlp, mlp_part, da_part,
        (mlp_base, near_a, near_b, far_a, far_b), upb_other,
    )
    da_peers = [links.core(part) for part in da_parts]
    gated, grad_upper, down_got, up_got = lax.optimization_barrier(
        (gated, grad_upper, down_got, up_got)
    )
    down.take(down_got)
    up.take(up_got)
    down_other = Reduction(links, dot(dmlp, gated, 0, 0))
    up_other = Reduction(links, dot(a_second, grad_upper, 0, 0))
    down_sent, up_sent = down_other.send(0), up_other.send(1)
    down_got, up_got = links.data(down_sent, 0), links.data(up_sent, 1)
    def my_rows(array):
        return lax.dynamic_slice_in_dim(array, core * half_rows, half_rows, 0)

    def peer_rows(array):
        return lax.dynamic_slice_in_dim(array, (1 - core) * half_rows, half_rows, 0)

    mlp_sum = my_rows(mlp_part) + links.core(peer_rows(mlp_part))
    result_mine = my_rows(hidden) + mlp_sum
    result_far = links.half(result_mine)
    mlp_mine = mlp_sum + vec_params[5]
    mlp_sq = jnp.sum(my_rows(kept[:, :1]) * mlp_mine * mlp_mine)
    dh, dattn, do_own, do_other, row_sums = hidden_back(
        hold(hidden, down_sent, up_sent, result_mine), da_parts, da_peers, cot_win, kept, vec_params,
        out_weight, out_other,
    )

    *draws, own_sums = attention_back(plan, own, do_own, head_cols, kcode, qseg, heads, dim)
    down_other.take(hold(down_got, draws[1]))
    up_other.take(hold(up_got, draws[1]))
    down.array = jnp.concatenate([down.array, down_other.array], axis=-1)
    up.array = jnp.concatenate([up.array, up_other.array], axis=-1)
    down_sent, up_sent = down.send(1), up.send(0)
    down_got, up_got = links.data(down_sent, 1), links.data(up_sent, 0)
    result_near = links.core(result_mine)
    *draws, other_sums = attention_back(
        plan, other, hold(do_other, down_sent, up_sent, result_far, result_near), other_cols, kcode,
        qseg, heads, dim, draws,
    )
    down.take(hold(down_got, draws[1]))
    up.take(hold(up_got, draws[1]))
    mlp = Reduction(links, jnp.zeros((width, 1), F32))
    mlp.left = list(down.left)
    mlp_sent = jnp.concatenate([down.array[..., units:], up.array[..., units:]], axis=-1)
    mlp.kept = jnp.concatenate([down.array[..., :units], up.array[..., :units]], axis=-1)
    mlp_got = links.half(mlp_sent)
    result_far_near = links.core(hold(result_far, draws[1]))
    draws = lax.optimization_barrier((*draws, mlp_sent))[:2]
    qk_own, qk_other, value_out = last_gradients(a_first, dattn, *draws, own[6], other[6])
    last_bits = list(mlp.left)
    value_out = Reduction(links, value_out)
    value_out_sent = value_out.send(0)
    qk_got, value_out_got = links.half(qk_other), links.data(value_out_sent, 0)
    da1_part = dot(draws[0], qk_cat, 0, 0) + dot(draws[1], value_cat, 0, 0)
    da1_sent = peer_rows(da1_part)
    da1_peer = links.core(da1_sent)
    grad_left, grad_right, first_sums = input_back(
        jnp.full((1,), core, jnp.int32), hold(da1_part, result_far_near), da1_peer, x_win, dh, vec_params
    )
    grad_nears = [links.core(grad_left), links.core(grad_right)]
    far_left = links.half(grad_left)

    mlp.take(hold(mlp_got, grad_left))
    mlp_sent = mlp.send(last_bits[0])
    mlp_got = links.data(mlp_sent, last_bits[0])
    value_out.take(hold(value_out_got, grad_left))
    value_out_sent = value_out.send(1)
    value_out_got = links.data(value_out_sent, 1)
    rows = width // links.dp_size
    first_row = links.dp * rows
    old_shares = (
        lax.dynamic_slice_in_dim(qkv_weight, first_row, rows, 1),
        lax.dynamic_slice_in_dim(out_weight, first_row, rows, 1),
        lax.dynamic_slice_in_dim(up_weight, first_row, rows, 0),
        lax.dynamic_slice_in_dim(down_weight, first_row, rows, 1).T,
    )
    query_key = Reduction(links, qk_own + hold(qk_got, value_out_sent, *old_shares))
    query_key_sent = query_key.send(0)
    query_key_got = links.data(query_key_sent, 0)
    core_index = jnp.full((1,), core, jnp.int32)
    mine, away = pack_small(
        core_index, hold(first_sums, query_key_sent), row_sums, kept, attn_sums, mlp_sq.reshape(1),
        own_sums, other_sums, upb_sums, upb_sums_other,
    )
    summed = mine + links.half(away)
    value_out.take(hold(value_out_got, query_key_sent, mlp_got))
    value_out_sent = value_out.send("half")
    value_out_got = links.half(value_out_sent)
    one = jnp.ones((1,), F32)
    result = join_sequence(
        links, [(hold(result_mine, query_key_sent), result_near, result_far, result_far_near)], parting,
        seq_len, window, one, vec_params[5:6],
    )
    query_key.take(hold(query_key_got, summed, result, far_left))
    query_key_sent = query_key.send(1)
    query_key_got = links.data(query_key_sent, 1)
    summed = hold(summed, query_key_sent)
    shared = summed[:8]
    summed = jnp.concatenate([shared + links.core(shared), summed[8:]], axis=0)
    value_out_got = hold(value_out_got, query_key_sent)
    value_out.take(value_out_got)
    far_right = links.half(hold(grad_right, value_out_got))
    far_near_left = links.core(hold(far_left, value_out_got))
    query_key.take(hold(query_key_got, summed))
    last = Reduction(links, jnp.zeros((width, 1), F32))
    last.left = list(last_bits)
    last.array = jnp.concatenate([query_key.array, value_out.array], axis=-1)
    last_sent = last.send(last_bits[0])
    last_got = links.data(last_sent, last_bits[0])
    summed = hold(summed, last_sent)
    summed = links.sum_data(summed)
    mlp.take(mlp_got)
    for bit in last_bits[1:]:
        mlp.step(bit)
    last_got, summed = lax.optimization_barrier((last_got, summed))
    last.take(last_got)
    while last.left:
        last.step(last.left[0])
    last_share = last.array

    vec_grad = summed[:6]
    stats = summed[6, :3]
    tail = summed[8:].reshape(-1)
    head_grad = tail[: head_params.size].reshape(head_params.shape)
    head_rows = -(-own_sums.shape[1] // width)
    bup_grad = tail[head_rows * width : head_rows * width + units]
    count = stats[0]
    scale = seq_len * links.dp_size / count
    shares = (last_share, last_share, mlp.array, mlp.array)
    first_dp = links.dp == 0
    first_mp = links.mp == 0
    big_sq = jnp.sum(last_share * last_share) + jnp.sum(mlp.array * mlp.array)
    split_sq = jnp.sum(head_grad * head_grad) + jnp.sum(bup_grad * bup_grad)
    whole_sq = jnp.sum(vec_grad * vec_grad)
    raw_sq = (
        big_sq + jnp.where(first_dp, split_sq, 0.0) + jnp.where(first_dp & first_mp, whole_sq, 0.0)
    )
    sq_total = links.sum_all(raw_sq)
    grad_norm = scale * jnp.sqrt(sq_total)
    factor = jnp.minimum(1.0, CLIP_LIMIT / (grad_norm + 1e-06)) * scale
    steps_f = step_count[0].astype(F32)
    corr_one = 1.0 - BETA_ONE**steps_f
    corr_two = 1.0 - BETA_TWO**steps_f
    far_right = hold(far_right, sq_total)
    grad_input = join_sequence(
        links,
        [
            (grad_left, grad_nears[0], far_left, far_near_left),
            (grad_right, grad_nears[1], far_right, links.core(far_right)),
        ],
        parting, seq_len, window, scale.reshape(1), jnp.zeros((1, width), F32),
    )
    new_qkv, new_out, new_up, new_down, new_head, new_vec = update(
        jnp.stack([factor, corr_one, corr_two]),
        [
            (old_shares[0], shares[0], qkv_first, qkv_second),
            (old_shares[1], shares[1], out_first, out_second),
            (old_shares[2], shares[2], up_first, up_second),
            (old_shares[3], shares[3], down_first.T, down_second.T),
            (head_params, head_grad, head_first, head_second),
            (vec_params, vec_grad, vec_first, vec_second),
        ],
        (WEIGHT_DECAY,) * 4 + (0.0,) * 2,
    )
    new_down = [array.T for array in new_down]
    new_upb = adam_step(
        up_bias, bup_grad, upb_first, upb_second, factor, corr_one, corr_two, 0.0
    )
    rms = jnp.sqrt(stats[1:] / (count * width))
    return (
        result, grad_input, *new_qkv, *new_out, *new_up, *new_down, *new_head, *new_upb, *new_vec,
        grad_norm.reshape(1), rms,
    )


def solution(mesh):
    seq = P("dp", None, None)
    row = P("dp", None)
    qkv = P(None, "dp", "mp")
    out = P("mp", "dp")
    up = P("dp", "mp")
    head = P(None, "mp", None)
    unit = P("mp")
    whole = P()
    return jax.shard_map(
        local,
        mesh=mesh,
        in_specs=(
            *(seq, seq, row, row, whole),
            *(P(None, None, "mp"), qkv, qkv),
            *(P("mp", None), out, out),
            *(P(None, "mp"), up, up),
            *(P("mp", None), out, out),
            *(head, head, head),
            *(unit, unit, unit),
            *(whole, whole, whole),
        ),
        out_specs=(
            *(seq, seq),
            *(qkv, qkv, qkv),
            *(out, out, out),
            *(up, up, up),
            *(out, out, out),
            *(head, head, head),
            *(unit, unit, unit),
            *(whole, whole, whole),
            *(whole, whole),
        ),
        check_vma=False,
    )
```

profile of v0, /device:TPU:0, one launch (start us, length us, event | category | flops | bytes accessed | tf_op | source)
XLA Modules:
  0.0 377.7 jit_solution(2167041384783909236)
XLA Ops:
  10.0 8.8 %heads_own.1 = (bf16[1280,768]{1,0:T(8,128)(2,1)}, bf16[192,1280]{1,0:T(8,128)(2,1)}, bf16[192,1280]{1,0:T(8,128)(2,1)}, bf16[192,1280]{1,0:T(8,128)(2,1)}, bf16...) custom-call(bf16[1280,768]{1,0:T(8,128)(2,1)} %dynamic-slice_bitcast_fusion.1.x_ref, ...), custom_call_target="tpu_custom_call" | custom-call | flops 1132462080 | bytes 7864320 | tf_op jit(solution)/shard_map/heads_own/pallas_call | solution.py:355
  33.4 11.3 %attention.2 = (bf16[192,1280]{1,0:T(8,128)(2,1)}, f32[24,1280]{1,0:T(8,128)}) custom-call(s32[8,128]{1,0:T(8,128)} %copy-done.35, bf16[192,1280]{1,0:T(8,128)(2,1)} %get-tuple-element.149.q_ref, bf16[192,1280]{1,0:T(8,128)(2,1)} %get-tuple-element.150.k_ref, bf16[192,1280]{1,0:T(8,128)(2,1)} %get-tuple-element.151.v_ref, s32[1280,128]{1,0:T(8,128)} %copy-done.17, ...), custom_call_target="tpu_custom_call" | custom-call | flops 754974720 | bytes 1966080 | tf_op jit(solution)/shard_map/attention/pallas_call | solution.py:389
  45.5 7.6 %heads_other.1 = (bf16[192,1280]{1,0:T(8,128)(2,1)}, bf16[192,1280]{1,0:T(8,128)(2,1)}, bf16[192,1280]{1,0:T(8,128)(2,1)}, bf16[192,1280]{1,0:T(8,128)(2,1)}, bf...) custom-call(s32[4]{0:T(128)} %pad_add_fusion.1.spots_ref, ...), custom_call_target="tpu_custom_call" | custom-call | flops 1132462080 | bytes 7864320 | tf_op jit(solution)/shard_map/heads_other/pallas_call | solution.py:372
  59.8 11.3 %attention.3 = (bf16[192,1280]{1,0:T(8,128)(2,1)}, f32[24,1280]{1,0:T(8,128)}) custom-call(s32[8,128]{1,0:T(8,128)} %copy-done.35, bf16[192,1280]{1,0:T(8,128)(2,1)} %get-tuple-element.165.q_ref, bf16[192,1280]{1,0:T(8,128)(2,1)} %get-tuple-element.166.k_ref, bf16[192,1280]{1,0:T(8,128)(2,1)} %get-tuple-element.167.v_ref, s32[1280,128]{1,0:T(8,128)} %copy-done.17, ...), custom_call_target="tpu_custom_call" | custom-call | flops 754974720 | bytes 1966080 | tf_op jit(solution)/shard_map/attention/pallas_call | solution.py:389
  84.2 18.7 %mlp_own.1 = (f32[1280,768]{1,0:T(8,128)}, bf16[1280,768]{1,0:T(8,128)(2,1)}, bf16[1280,768]{1,0:T(8,128)(2,1)}, bf16[1280,768]{1,0:T(8,128)(2,1)}, bf16[1280,76...) custom-call(bf16[1280,768]{1,0:T(8,128)(2,1)} %dynamic-slice_bitcast_fusi, ...), custom_call_target="tpu_custom_call" | custom-call | flops 6039797760 | bytes 39321600 | tf_op jit(solution)/shard_map/mlp_own/pallas_call | solution.py:650
  102.9 4.1 %fusion.25 = f32[768,768]{1,0:T(8,128)S(1)} fusion(bf16[1280,768]{1,0:T(8,128)(2,1)} %get-tuple-element.177.a_ref, bf16[1280,768]{1,0:T(8,128)(2,1)} %get-tuple-element.176), kind=kOutput, calls=%fused_computation.93 | convolution fusion | flops 1509949440 | bytes 6291456 | tf_op jit(solution)/shard_map/dot_general | solution.py:33
  116.1 16.1 %mlp_other.1 = (bf16[1280,768]{1,0:T(8,128)(2,1)}, bf16[1280,768]{1,0:T(8,128)(2,1)}, f32[1280,768]{1,0:T(8,128)}, f32[1280,384]{1,0:T(8,128)}, f32[1280,384]{1,0:T(8,128)}, /*index=5*/f32[1,768]{1,0:T(1,128)}) custom-call(s32[4]{0:T(128)} %pad_add_fusion.1.spots_ref, bf16[1280,768]{1,0:T(8,128)(2,1)} %get-tuple-element.177.a_ref, ...), custom_call_target="tpu_custom_call", output_to_operand_aliasing={{2}: (3, {})} | custom-call | flops 6039797760 | bytes 27525120 | tf_op jit(solution)/shard_map/mlp_other/pallas_call | solution.py:688
  136.7 5.6 %collective-permute-done.13 = f32[2,2,96,768]{3,2,1,0:T(8,128)} collective-permute-done((f32[2,2,96,768]{3,2,1,0:T(8,128)}, f32[2,2,96,768]{3,2,1,0:T(8,128)}, u32[]{:S(2)}, u32[]{:S(2)}) %collective-permute-start.13) | collective-permute-done | bytes 1179680 | tf_op jit(solution)/shard_map/ppermute | solution.py:53
  142.3 4.0 %fusion.26 = f32[768,768]{1,0:T(8,128)S(1)} fusion(bf16[1280,768]{1,0:T(8,128)(2,1)} %get-tuple-element.174.dmlp_ref, bf16[1280,768]{1,0:T(8,128)(2,1)} %get-tuple-element.185), kind=kOutput, calls=%fused_computation.94 | convolution fusion | flops 1509949440 | bytes 6291456 | tf_op jit(solution)/shard_map/dot_general | solution.py:33
  157.2 6.9 %hidden_back.1 = (f32[1280,768]{1,0:T(8,128)S(1)}, bf16[1280,768]{1,0:T(8,128)(2,1)S(1)}, bf16[192,1280]{1,0:T(8,128)(2,1)S(1)}, bf16[192,1280]{1,0:T(8,128)(2,1)S(1)}, f32[4,768]{1,0:T(4,128)S(1)}) custom-call(f32[1280,768]{1,0:T(8,128)S(1)} %copy-done.2, f32[1280,384]{1,0:T(8,128)} %get-tuple-element.188.mine_left, f32[1280,384]{1,0:T(8,128)S(1)} %copy-done.11, ...), custom_call_target="tpu_custom_call" | custom-call | flops 754974720 | bytes 21626880 | tf_op jit(solution)/shard_map/hidden_back/pallas_call | solution.py:757
  164.2 15.1 %attention_back.2 = (bf16[768,1280]{1,0:T(8,128)(2,1)S(1)}, bf16[384,1280]{1,0:T(8,128)(2,1)S(1)}, f32[1,1024]{1,0:T(1,128)S(1)}) custom-call(s32[8,128]{1,0:T(8,128)S(1)} %copy-done.36, bf16[192,1280]{1,0:T(8,128)(2,1)S(1)} %copy-done.41, bf16[192,1280]{1,0:T(8,128)(2,1)S(1)} %copy-done.42, bf16[192,1280]{1,0:T(8,128)(2,1)S(1)} %copy-done.43, ...), custom_call_target="tpu_custom_call" | custom-call | flops 1887436800 | bytes 7372800 | tf_op jit(solution)/shard_map/attention_back/pallas_call | solution.py:512
  183.2 15.1 %collective-permute-done.19.refs_2_ = f32[640,768]{1,0:T(8,128)} collective-permute-done((f32[640,768]{1,0:T(8,128)S(1)}, f32[640,768]{1,0:T(8,128)}, u32[]{:S(2)}, u32[]{:S(2)}) %collective-permute-start.19) | collective-permute-done | bytes 1966112 | tf_op jit(solution)/shard_map/ppermute | solution.py:50
  198.3 15.3 %attention_back.3 = (bf16[768,1280]{1,0:T(8,128)(2,1)S(1)}, bf16[384,1280]{1,0:T(8,128)(2,1)S(1)}, f32[1,1024]{1,0:T(1,128)S(1)}) custom-call(s32[8,128]{1,0:T(8,128)S(1)} %copy-done.36, bf16[192,1280]{1,0:T(8,128)(2,1)S(1)} %copy-done.21, bf16[192,1280]{1,0:T(8,128)(2,1)S(1)} %copy-done.22, ...), custom_call_target="tpu_custom_call", output_to_operand_aliasing={{0}: (13, {}), {1}: (14, {})} | custom-call | flops 1887436800 | bytes 7372800 | tf_op jit(solution)/shard_map/attention_back/pallas_call | solution.py:512
  223.2 4.3 %last_gradients.1 = (f32[768,384]{1,0:T(8,128)S(1)}, f32[768,384]{1,0:T(8,128)S(1)}, f32[768,768]{1,0:T(8,128)S(1)}) custom-call(bf16[1280,768]{1,0:T(8,128)(2,1)S(1)} %copy-done.10, bf16[1280,768]{1,0:T(8,128)(2,1)S(1)} %get-tuple-element.190.dattn_ref, bf16[768,1280]{1,0:T(8,128)(2,1)S(1)} %get-tuple-element.212.qk_ref, ...), custom_call_target="tpu_custom_call" | custom-call | flops 3019898880 | bytes 11796480 | tf_op jit(solution)/shard_map/last_gradients/pallas_call | solution.py:848
  234.8 6.3 %input_back.1 = (f32[640,384]{1,0:T(8,128)}, f32[640,384]{1,0:T(8,128)}, f32[2,768]{1,0:T(2,128)}) custom-call(s32[1]{0:T(128)} %bitcast.core_ref, f32[1280,768]{1,0:T(8,128)} %copy-done.48, f32[640,768]{1,0:T(8,128)} %collective-permute-done.26.peer_ref, bf16[1280,768]{1,0:T(8,128)(2,1)} %dynamic-slice_bitcast_fusion.1.x_ref, f32[1280,768]{1,0:T(8,128)} %copy-done.6, ...), custom_call_target="tpu_custom_call" | custom-call | bytes 8847360 | tf_op jit(solution)/shard_map/input_back/pallas_call | solution.py:809
  241.2 11.2 %collective-permute-done.33 = f32[2,96,1536]{2,1,0:T(8,128)} collective-permute-done((f32[2,96,1536]{2,1,0:T(8,128)}, f32[2,96,1536]{2,1,0:T(8,128)}, u32[]{:S(2)}, u32[]{:S(2)}) %collective-permute-start.33) | collective-permute-done | bytes 1179680 | tf_op jit(solution)/shard_map/ppermute | solution.py:50
  266.2 11.5 %collective-permute-done.23 = f32[768,384]{1,0:T(8,128)} collective-permute-done((f32[768,384]{1,0:T(8,128)}, f32[768,384]{1,0:T(8,128)}, u32[]{:S(2)}, u32[]{:S(2)}) %collective-permute-start.23) | collective-permute-done | bytes 1179680 | tf_op jit(solution)/shard_map/ppermute | solution.py:50
  282.9 6.8 %join_sequence.2 = bf16[1,2048,768]{2,1,0:T(8,128)(2,1)} custom-call(s32[3]{0:T(128)} %pad_add_fusion.info_ref, f32[1]{0:T(128)} %constant.142.clone.1.factor_ref, f32[1,768]{1,0:T(1,128)} %get-tuple-element.291.shift_ref, f32[640,768]{1,0:T(8,128)} %copy-done.53, f32[640,768]{1,0:T(8,128)} %copy-done.64, f32[640,768]{1,0:T(8,128)} %collective-permute-done.19.refs_2_, ...), custom_call_target="tpu_custom_call" | custom-call | bytes 11010048 | tf_op jit(solution)/shard_map/join_sequence/pallas_call | solution.py:999
  289.7 9.0 %collective-permute-done.28 = f32[16,768]{1,0:T(8,128)S(1)} collective-permute-done((f32[16,768]{1,0:T(8,128)S(1)}, f32[16,768]{1,0:T(8,128)S(1)}, u32[]{:S(2)}, u32[]{:S(2)}) %collective-permute-start.28) | collective-permute-done | bytes 49184 | tf_op jit(solution)/shard_map/ppermute | solution.py:50
  301.5 6.6 %collective-permute-done.35 = f32[2,96,384]{2,1,0:T(8,128)S(1)} collective-permute-done((f32[2,96,384]{2,1,0:T(8,128)S(1)}, f32[2,96,384]{2,1,0:T(8,128)S(1)}, u32[]{:S(2)}, u32[]{:S(2)}) %collective-permute-start.35) | collective-permute-done | bytes 294944 | tf_op jit(solution)/shard_map/ppermute | solution.py:50
  309.9 4.1 %collective-permute-done.37 = f32[16,768]{1,0:T(8,128)S(1)} collective-permute-done((f32[16,768]{1,0:T(8,128)S(1)}, f32[16,768]{1,0:T(8,128)S(1)}, u32[]{:S(2)}, u32[]{:S(2)}) %collective-permute-start.37) | collective-permute-done | bytes 49184 | tf_op jit(solution)/shard_map/ppermute | solution.py:53
  322.5 8.5 %collective-permute-done.39 = f32[16,768]{1,0:T(8,128)S(1)} collective-permute-done((f32[16,768]{1,0:T(8,128)S(1)}, f32[16,768]{1,0:T(8,128)S(1)}, u32[]{:S(2)}, u32[]{:S(2)}) %collective-permute-start.39) | collective-permute-done | bytes 49184 | tf_op jit(solution)/shard_map/ppermute | solution.py:53
  362.8 4.4 %update.1 = (f32[3,96,192]{2,1,0:T(8,128)}, f32[3,96,192]{2,1,0:T(8,128)}, f32[3,96,192]{2,1,0:T(8,128)}, f32[192,96]{1,0:T(8,128)}, f32[192,96]{1,0:T(8,128)}, ...) custom-call(f32[3]{0:T(128)} %pad_maximum_fusion.5.refs_0_, ...), custom_call_target="tpu_custom_call" | custom-call | bytes 6349056 | tf_op jit(solution)/shard_map/update/pallas_call | solution.py:936
  369.5 7.1 %join_sequence.3 = bf16[1,2048,768]{2,1,0:T(8,128)(2,1)} custom-call(s32[3]{0:T(128)} %pad_add_fusion.info_ref, f32[1]{0:T(128)} %bitcast.50.factor_ref, f32[1,768]{1,0:T(1,128)} %broadcast_in_dim.2.shift_ref, f32[640,384]{1,0:T(8,128)} %get-tuple-element.222.refs_0_, f32[640,384]{1,0:T(8,128)} %collective-permute-done.40.refs_1_, ...), custom_call_target="tpu_custom_call" | custom-call | bytes 11010048 | tf_op jit(solution)/shard_map/join_sequence/pallas_call | solution.py:999
  (334 shorter events, 146.9 us)
Async XLA Ops:
  21.1 32.0 %collective-permute-start.5 = (f32[2,192,768]{2,1,0:T(8,128)}, f32[2,192,768]{2,1,0:T(8,128)S(1)}, u32[]{:S(2)}, u32[]{:S(2)}) collective-permute-start(f32[2,192,768]{2,1,0:T(8,128)} %fusion.11), channel_id=1, source_target_pairs={{0,2},{1,3},{2,0},{3,1},{4,6},{5,7},{6,4},{7,5},{8,10},{9,11},{10,... | collective-permute-start | bytes 3538952 | tf_op jit(solution)/shard_map/ppermute | solution.py:50
  23.1 21.6 %collective-permute-start.1 = (f32[3,48,768]{2,1,0:T(8,128)}, f32[3,48,768]{2,1,0:T(8,128)S(1)}, u32[]{:S(2)}, u32[]{:S(2)}) collective-permute-start(f32[3,48,768]{2,1,0:T(8,128)} %collective-permute-done.p0), channel_id=1, source_target_pairs={{0,4},{4,0},{8,12},{12,8},{16,20},{20,16},{24,28},{28,24},{1,5},{5... | collective-permute-start | bytes 1327112 | tf_op jit(solution)/shard_map/ppermute | solution.py:53
  80.4 34.7 %collective-permute-start.10 = (f32[2,2,96,768]{3,2,1,0:T(8,128)}, f32[2,2,96,768]{3,2,1,0:T(8,128)}, u32[]{:S(2)}, u32[]{:S(2)}) collective-permute-start(f32[2,2,96,768]{3,2,1,0:T(8,128)} %pad_maximum_fusion), channel_id=1, source_target_pairs={{0,8},{4,12},{8,0},{12,4},{16,24},{20,28},{24,16},{28,20},{1,9},{5... | collective-permute-start | bytes 3538952 | tf_op jit(solution)/shard_map/ppermute | solution.py:53
  83.2 31.9 %collective-permute-start.11 = (f32[2,2,96,768]{3,2,1,0:T(8,128)}, f32[2,2,96,768]{3,2,1,0:T(8,128)S(1)}, u32[]{:S(2)}, u32[]{:S(2)}) collective-permute-start(f32[2,2,96,768]{3,2,1,0:T(8,128)} %pad_maximum_fusion.1), channel_id=1, source_target_pairs={{0,4},{4,0},{8,12},{12,8},{16,20},{20,16},{24,28},{28,24},{1,5},{5... | collective-permute-start | bytes 3538952 | tf_op jit(solution)/shard_map/ppermute | solution.py:53
  108.2 28.5 %collective-permute-start.14 = (f32[2,2,96,768]{3,2,1,0:T(8,128)}, f32[2,2,96,768]{3,2,1,0:T(8,128)}, u32[]{:S(2)}, u32[]{:S(2)}) collective-permute-start(f32[2,2,96,768]{3,2,1,0:T(8,128)} %dynamic-slice_bitcast_fusion.5), channel_id=1, source_target_pairs={{0,8},{4,12},{8,0},{12,4},{16,24},{20,28},{24,16},{28,20},{1,9},{5... | collective-permute-start | bytes 3538952 | tf_op jit(solution)/shard_map/ppermute | solution.py:53
  114.1 28.1 %collective-permute-start.13 = (f32[2,2,96,768]{3,2,1,0:T(8,128)}, f32[2,2,96,768]{3,2,1,0:T(8,128)}, u32[]{:S(2)}, u32[]{:S(2)}) collective-permute-start(f32[2,2,96,768]{3,2,1,0:T(8,128)} %dynamic-slice_bitcast_fusion.6), channel_id=1, source_target_pairs={{0,4},{4,0},{8,12},{12,8},{16,20},{20,16},{24,28},{28,24},{1,5},{5... | collective-permute-start | bytes 3538952 | tf_op jit(solution)/shard_map/ppermute | solution.py:53
  136.0 21.1 %collective-permute-start.16 = (f32[1280,384]{1,0:T(8,128)}, f32[1280,384]{1,0:T(8,128)S(1)}, u32[]{:S(2)}, u32[]{:S(2)}) collective-permute-start(f32[1280,384]{1,0:T(8,128)} %get-tuple-element.189.mine_right), channel_id=1, source_target_pairs={{0,1},{1,0},{2,3},{3,2},{4,5},{5,4},{6,7},{7,6},{8,9},{9,8},{10,11... | collective-permute-start | bytes 5898248 | tf_op jit(solution)/shard_map/ppermute | solution.py:47
  146.4 32.9 %collective-permute-start.17 = (f32[2,2,96,768]{3,2,1,0:T(8,128)S(1)}, f32[2,2,96,768]{3,2,1,0:T(8,128)S(1)}, u32[]{:S(2)}, u32[]{:S(2)}) collective-permute-start(f32[2,2,96,768]{3,2,1,0:T(8,128)S(1)} %dynamic-slice_bitcast_fusion.4), channel_id=1, source_target_pairs={{0,4},{4,0},{8,12},{12,8},{16,20},{20,16},{24,28},{28,24},{1,5},{5... | collective-permute-start | bytes 3538952 | tf_op jit(solution)/shard_map/ppermute | solution.py:53
  149.7 32.9 %collective-permute-start.18 = (f32[2,2,96,768]{3,2,1,0:T(8,128)S(1)}, f32[2,2,96,768]{3,2,1,0:T(8,128)S(1)}, u32[]{:S(2)}, u32[]{:S(2)}) collective-permute-start(f32[2,2,96,768]{3,2,1,0:T(8,128)S(1)} %dynamic-slice_bitcast_fusion.3), channel_id=1, source_target_pairs={{0,8},{4,12},{8,0},{12,4},{16,24},{20,28},{24,16},{28,20},{1,9},{5... | collective-permute-start | bytes 3538952 | tf_op jit(solution)/shard_map/ppermute | solution.py:53
  154.3 43.9 %collective-permute-start.19 = (f32[640,768]{1,0:T(8,128)S(1)}, f32[640,768]{1,0:T(8,128)}, u32[]{:S(2)}, u32[]{:S(2)}) collective-permute-start(f32[640,768]{1,0:T(8,128)S(1)} %get-tuple-element.225.refs_0_), channel_id=1, source_target_pairs={{0,2},{1,3},{2,0},{3,1},{4,6},{5,7},{6,4},{7,5},{8,10},{9,11},{10,... | collective-permute-start | bytes 5898248 | tf_op jit(solution)/shard_map/ppermute | solution.py:50
  154.7 43.5 %collective-permute-start.20 = (f32[640,768]{1,0:T(8,128)S(1)}, f32[640,768]{1,0:T(8,128)S(1)}, u32[]{:S(2)}, u32[]{:S(2)}) collective-permute-start(f32[640,768]{1,0:T(8,128)S(1)} %get-tuple-element.225.refs_0_), channel_id=1, source_target_pairs={{0,1},{1,0},{2,3},{3,2},{4,5},{5,4},{6,7},{7,6},{8,9},{9,8},{10,11... | collective-permute-start | bytes 5898248 | tf_op jit(solution)/shard_map/ppermute | solution.py:47
  179.7 34.0 %collective-permute-start.21 = (f32[2,96,1536]{2,1,0:T(8,128)S(1)}, f32[2,96,1536]{2,1,0:T(8,128)S(1)}, u32[]{:S(2)}, u32[]{:S(2)}) collective-permute-start(f32[2,96,1536]{2,1,0:T(8,128)S(1)} %fusion.10), channel_id=1, source_target_pairs={{0,8},{4,12},{8,0},{12,4},{16,24},{20,28},{24,16},{28,20},{1,9},{5... | collective-permute-start | bytes 3538952 | tf_op jit(solution)/shard_map/ppermute | solution.py:53
  183.1 31.6 %collective-permute-start.22 = (f32[2,96,1536]{2,1,0:T(8,128)S(1)}, f32[2,96,1536]{2,1,0:T(8,128)S(1)}, u32[]{:S(2)}, u32[]{:S(2)}) collective-permute-start(f32[2,96,1536]{2,1,0:T(8,128)S(1)} %fusion.5), channel_id=1, source_target_pairs={{0,4},{4,0},{8,12},{12,8},{16,20},{20,16},{24,28},{28,24},{1,5},{5... | collective-permute-start | bytes 3538952 | tf_op jit(solution)/shard_map/ppermute | solution.py:53
  223.2 29.2 %collective-permute-start.33 = (f32[2,96,1536]{2,1,0:T(8,128)}, f32[2,96,1536]{2,1,0:T(8,128)}, u32[]{:S(2)}, u32[]{:S(2)}) collective-permute-start(f32[2,96,1536]{2,1,0:T(8,128)} %pad_maximum_fusion.2), channel_id=1, source_target_pairs={{0,2},{1,3},{2,0},{3,1},{4,6},{5,7},{6,4},{7,5},{8,10},{9,11},{10,... | collective-permute-start | bytes 3538952 | tf_op jit(solution)/shard_map/ppermute | solution.py:50
  230.2 28.5 %collective-permute-start.24 = (f32[2,2,96,768]{3,2,1,0:T(8,128)}, f32[2,2,96,768]{3,2,1,0:T(8,128)}, u32[]{:S(2)}, u32[]{:S(2)}) collective-permute-start(f32[2,2,96,768]{3,2,1,0:T(8,128)} %dynamic-slice_bitcast_fusion.2), channel_id=1, source_target_pairs={{0,4},{4,0},{8,12},{12,8},{16,20},{20,16},{24,28},{28,24},{1,5},{5... | collective-permute-start | bytes 3538952 | tf_op jit(solution)/shard_map/ppermute | solution.py:53
  232.7 45.0 %collective-permute-start.23 = (f32[768,384]{1,0:T(8,128)}, f32[768,384]{1,0:T(8,128)}, u32[]{:S(2)}, u32[]{:S(2)}) collective-permute-start(f32[768,384]{1,0:T(8,128)} %copy-done.40), channel_id=1, source_target_pairs={{0,2},{1,3},{2,0},{3,1},{4,6},{5,7},{6,4},{7,5},{8,10},{9,11},{10,... | collective-permute-start | bytes 3538952 | tf_op jit(solution)/shard_map/ppermute | solution.py:50
  241.1 59.2 %collective-permute-start.29 = (f32[640,384]{1,0:T(8,128)}, f32[640,384]{1,0:T(8,128)}, u32[]{:S(2)}, u32[]{:S(2)}) collective-permute-start(f32[640,384]{1,0:T(8,128)} %get-tuple-element.222.refs_0_), channel_id=1, source_target_pairs={{0,2},{1,3},{2,0},{3,1},{4,6},{5,7},{6,4},{7,5},{8,10},{9,11},{10,... | collective-permute-start | bytes 2949128 | tf_op jit(solution)/shard_map/ppermute | solution.py:50
  255.2 43.5 %collective-permute-start.34 = (f32[96,1536]{1,0:T(8,128)}, f32[96,1536]{1,0:T(8,128)}, u32[]{:S(2)}, u32[]{:S(2)}) collective-permute-start(f32[96,1536]{1,0:T(8,128)} %dynamic-slice_bitcast_fusion.7), channel_id=1, source_target_pairs={{0,16},{4,20},{8,24},{12,28},{16,0},{20,4},{24,8},{28,12},{1,17},{... | collective-permute-start | bytes 1769480 | tf_op jit(solution)/shard_map/ppermute | solution.py:53
  262.0 36.7 %collective-permute-start.32 = (f32[2,96,768]{2,1,0:T(8,128)}, f32[2,96,768]{2,1,0:T(8,128)}, u32[]{:S(2)}, u32[]{:S(2)}) collective-permute-start(f32[2,96,768]{2,1,0:T(8,128)} %dynamic-slice_bitcast_fusion.9), channel_id=1, source_target_pairs={{0,8},{4,12},{8,0},{12,4},{16,24},{20,28},{24,16},{28,20},{1,9},{5... | collective-permute-start | bytes 1769480 | tf_op jit(solution)/shard_map/ppermute | solution.py:53
  280.1 20.2 %collective-permute-start.27 = (f32[2,2,96,384]{3,2,1,0:T(8,128)}, f32[2,2,96,384]{3,2,1,0:T(8,128)}, u32[]{:S(2)}, u32[]{:S(2)}) collective-permute-start(f32[2,2,96,384]{3,2,1,0:T(8,128)} %dynamic-slice_bitcast_fusion.8), channel_id=1, source_target_pairs={{0,4},{4,0},{8,12},{12,8},{16,20},{20,16},{24,28},{28,24},{1,5},{5... | collective-permute-start | bytes 1769480 | tf_op jit(solution)/shard_map/ppermute | solution.py:53
  316.0 51.8 %collective-permute-start.40 = (f32[640,384]{1,0:T(8,128)}, f32[640,384]{1,0:T(8,128)}, u32[]{:S(2)}, u32[]{:S(2)}) collective-permute-start(f32[640,384]{1,0:T(8,128)} %get-tuple-element.222.refs_0_), channel_id=1, source_target_pairs={{0,1},{1,0},{2,3},{3,2},{4,5},{5,4},{6,7},{7,6},{8,9},{9,8},{10,11... | collective-permute-start | bytes 2949128 | tf_op jit(solution)/shard_map/ppermute | solution.py:47
  316.0 51.8 %collective-permute-start.42 = (f32[640,384]{1,0:T(8,128)}, f32[640,384]{1,0:T(8,128)}, u32[]{:S(2)}, u32[]{:S(2)}) collective-permute-start(f32[640,384]{1,0:T(8,128)} %get-tuple-element.246.refs_4_), channel_id=1, source_target_pairs={{0,1},{1,0},{2,3},{3,2},{4,5},{5,4},{6,7},{7,6},{8,9},{9,8},{10,11... | collective-permute-start | bytes 2949128 | tf_op jit(solution)/shard_map/ppermute | solution.py:47
  316.6 42.3 %collective-permute-start.43 = (f32[640,384]{1,0:T(8,128)}, f32[640,384]{1,0:T(8,128)S(1)}, u32[]{:S(2)}, u32[]{:S(2)}) collective-permute-start(f32[640,384]{1,0:T(8,128)} %get-tuple-element.246.refs_4_), channel_id=1, source_target_pairs={{0,2},{1,3},{2,0},{3,1},{4,6},{5,7},{6,4},{7,5},{8,10},{9,11},{10,... | collective-permute-start | bytes 2949128 | tf_op jit(solution)/shard_map/ppermute | solution.py:50
  331.0 36.9 %collective-permute-start.41 = (f32[640,384]{1,0:T(8,128)}, f32[640,384]{1,0:T(8,128)S(1)}, u32[]{:S(2)}, u32[]{:S(2)}) collective-permute-start(f32[640,384]{1,0:T(8,128)} %collective-permute-done.29.refs_2_), channel_id=1, source_target_pairs={{0,1},{1,0},{2,3},{3,2},{4,5},{5,4},{6,7},{7,6},{8,9},{9,8},{10,11... | collective-permute-start | bytes 2949128 | tf_op jit(solution)/shard_map/ppermute | solution.py:47
  (103 other events, 782.0 us)
where the time goes:
time: 379 us; the launch traced here: 378 us
  Pallas kernels  146 us (39%)
  waiting for transfers between devices  84.9 us (22%)
  local copies, waits for them, and re-layouts  49.6 us (13%)
  starting transfers between devices  37.7 us (10%)
  other arithmetic  34.1 us (9%)
  matrix products  14.6 us (4%)
  between operations  11.3 us (3%)
    ppermute x12, waiting for transfers between devices, half(): return lax.ppermute(array, 'mp', [(i, i ^ 2) for i in range(self.mp_size)])  55.7 us
    pallas_call x2, Pallas kernels, attention_back(): pl.pallas_call(functools.partial(attention_back_kernel, heads, dim), grid...  30.4 us
    ppermute x24, waiting for transfers between devices, data(): lax.ppermute(array, 'dp', [(i, i ^ 1 << bit) for i in range(self.dp_size)])  27.6 us
    pallas_call x2, Pallas kernels, attention(): pl.pallas_call(functools.partial(attention_kernel, heads, dim), out_shape...  22.6 us
    ppermute x24, starting transfers between devices, data(): lax.ppermute(array, 'dp', [(i, i ^ 1 << bit) for i in range(self.dp_size)])  22.2 us
    pallas_call x1, Pallas kernels, own_mlp(): pl.pallas_call(own_mlp_kernel, grid=(tokens // BLOCK,), out_shape=[struct...  18.7 us
    unnamed x157, local copies, waits for them, and re-layouts  17 us
    pallas_call x1, Pallas kernels, other_mlp(): pl.pallas_call(other_mlp_kernel, grid=(tokens // BLOCK,), out_shape=[stru...  16.1 us
  transfers between devices with their start and end apart: 50, of which 18 were waited for; matrix products, arithmetic and copies ran while one was open for 20% of the time, Pallas kernels for 36%

commit v1 on v0

--- a/solution.py
+++ b/solution.py
@@ -949,16 +949,26 @@
     seq_len = out_ref.shape[1]
     core, half, parting = info_ref[0], info_ref[1], info_ref[2]
     factor = factor_ref[0]
-    step = LANES
+    step, small = LANES, LANES // 4
     offset = seq_len - window
     start = 0
     for piece in range(pieces):
-        mine_ref, near_ref, far_ref, far_near_ref = refs[4 * piece : 4 * piece + 4]
-        cols = slice(start, start + mine_ref.shape[1])
-        start += mine_ref.shape[1]
+        far_cols = refs[4 * piece + 2].shape[-1]
+        cols = slice(start, start + far_cols)
+        start += far_cols
         shift = shift_ref[:, cols]
 
-        def rows_of(which, row, mine=mine_ref, near=near_ref, far=far_ref, far_near=far_near_ref):
+        def view(ref, piece=piece, cols=cols):
+            if len(ref.shape) == 3:
+                return ref.at[piece]
+            return ref if ref.shape[1] == cols.stop - cols.start else ref.at[:, cols]
+
+        mine_ref, near_ref, far_ref, far_near_ref = (
+            view(ref) for ref in refs[4 * piece : 4 * piece + 4]
+        )
+
+        def rows_of(which, row, step, views=(mine_ref, near_ref, far_ref, far_near_ref)):
+            mine, near, far, far_near = views
             from_core = row // half_rows
             spot = pl.ds(pl.multiple_of(row - from_core * half_rows, step), step)
             same = core == from_core
@@ -968,26 +978,27 @@
                 jnp.where(same, far[spot, :], far_near[spot, :]),
             )
 
-        def store(row, values, cols=cols, shift=shift):
+        def store(row, step, values, cols=cols, shift=shift):
             spot = pl.ds(pl.multiple_of(row, step), step)
             out_ref[0, spot, cols] = (values * factor + shift).astype(BF16)
 
         def first(block, carry, rows_of=rows_of, store=store):
-            store(block * step, rows_of(0, block * step))
+            store(block * step, step, rows_of(0, block * step, step))
             return carry
 
         def middle(block, carry, rows_of=rows_of, store=store):
-            row = block * step
-            places = row + lax.broadcasted_iota(jnp.int32, (step, 1), 0)
-            store(row, jnp.where(places < parting, rows_of(0, row), rows_of(1, row - offset)))
+            row = block * small
+            places = row + lax.broadcasted_iota(jnp.int32, (small, 1), 0)
+            one, two = rows_of(0, row, small), rows_of(1, row - offset, small)
+            store(row, small, jnp.where(places < parting, one, two))
             return carry
 
         def second(block, carry, rows_of=rows_of, store=store):
-            store(block * step, rows_of(1, block * step - offset))
+            store(block * step, step, rows_of(1, block * step - offset, step))
             return carry
 
         lax.fori_loop(0, offset // step, first, 0)
-        lax.fori_loop(offset // step, window // step, middle, 0)
+        lax.fori_loop(offset // small, window // small, middle, 0)
         lax.fori_loop(window // step, seq_len // step, second, 0)
 
 
@@ -1100,7 +1111,8 @@
 
     mlp_sum = my_rows(mlp_part) + links.core(peer_rows(mlp_part))
     result_mine = my_rows(hidden) + mlp_sum
-    result_far = links.half(result_mine)
+    cut = width // 2
+    result_far = [links.half(result_mine[:, :cut])]
     mlp_mine = mlp_sum + vec_params[5]
     mlp_sq = jnp.sum(my_rows(kept[:, :1]) * mlp_mine * mlp_mine)
     dh, dattn, do_own, do_other, row_sums = hidden_back(
@@ -1116,8 +1128,9 @@
     down_sent, up_sent = down.send(1), up.send(0)
     down_got, up_got = links.data(down_sent, 1), links.data(up_sent, 0)
     result_near = links.core(result_mine)
+    result_far.append(links.half(hold(result_mine, draws[1])[:, cut:]))
     *draws, other_sums = attention_back(
-        plan, other, hold(do_other, down_sent, up_sent, result_far, result_near), other_cols, kcode,
+        plan, other, hold(do_other, down_sent, up_sent, result_far[0], result_near), other_cols, kcode,
         qseg, heads, dim, draws,
     )
     down.take(hold(down_got, draws[1]))
@@ -1127,8 +1140,9 @@
     mlp_sent = jnp.concatenate([down.array[..., units:], up.array[..., units:]], axis=-1)
     mlp.kept = jnp.concatenate([down.array[..., :units], up.array[..., :units]], axis=-1)
     mlp_got = links.half(mlp_sent)
-    result_far_near = links.core(hold(result_far, draws[1]))
-    draws = lax.optimization_barrier((*draws, mlp_sent))[:2]
+    *draws, _, result_right = lax.optimization_barrier((*draws, mlp_sent, result_far[1]))
+    result_far[1] = result_right
+    result_far_near = links.core(jnp.stack(result_far))
     qk_own, qk_other, value_out = last_gradients(a_first, dattn, *draws, own[6], other[6])
     last_bits = list(mlp.left)
     value_out = Reduction(links, value_out)
@@ -1170,8 +1184,9 @@
     value_out_sent = value_out.send("half")
     value_out_got = links.half(value_out_sent)
     one = jnp.ones((1,), F32)
+    result_mine = hold(result_mine, query_key_sent)
     result = join_sequence(
-        links, [(hold(result_mine, query_key_sent), result_near, result_far, result_far_near)], parting,
+        links, [(result_mine, result_near, far, result_far_near) for far in result_far], parting,
         seq_len, window, one, vec_params[5:6],
     )
     query_key.take(hold(query_key_got, summed, result, far_left))
@@ -1213,23 +1228,26 @@
     first_dp = links.dp == 0
     first_mp = links.mp == 0
     big_sq = jnp.sum(last_share * last_share) + jnp.sum(mlp.array * mlp.array)
-    split_sq = jnp.sum(head_grad * head_grad) + jnp.sum(bup_grad * bup_grad)
-    whole_sq = jnp.sum(vec_grad * vec_grad)
+    split_sq = jnp.sum(summed[8:] * summed[8:])
+    whole_sq = jnp.sum(summed[:6] * summed[:6])
     raw_sq = (
         big_sq + jnp.where(first_dp, split_sq, 0.0) + jnp.where(first_dp & first_mp, whole_sq, 0.0)
     )
-    sq_total = links.sum_all(raw_sq)
+    raw_sq = raw_sq + links.core(raw_sq)
+    raw_sq = raw_sq + links.half(raw_sq)
+    far_right = hold(far_right, raw_sq)
+    far_near_right = links.core(far_right)
+    sq_total = links.sum_data(raw_sq)
     grad_norm = scale * jnp.sqrt(sq_total)
     factor = jnp.minimum(1.0, CLIP_LIMIT / (grad_norm + 1e-06)) * scale
     steps_f = step_count[0].astype(F32)
     corr_one = 1.0 - BETA_ONE**steps_f
     corr_two = 1.0 - BETA_TWO**steps_f
-    far_right = hold(far_right, sq_total)
     grad_input = join_sequence(
         links,
         [
             (grad_left, grad_nears[0], far_left, far_near_left),
-            (grad_right, grad_nears[1], far_right, links.core(far_right)),
+            (grad_right, grad_nears[1], far_right, far_near_right),
         ],
         parting, seq_len, window, scale.reshape(1), jnp.zeros((1, width), F32),
     )

time: 379 us -> 376 us (level)
  starting transfers between devices: 37.7 us -> 63 us
  waiting for transfers between devices: 84.9 us -> 65.2 us
  Pallas kernels: 146 us -> 138 us
    ppermute x12 -> x13, waiting for transfers between devices: 55.7 us -> 27.4 us  [half(): return lax.ppermute(array, 'mp', [(i, i ^ 2) for i in range(self.mp_size)])]
    ppermute x24, starting transfers between devices: 22.2 us -> 39.6 us  [data(): lax.ppermute(array, 'dp', [(i, i ^ 1 << bit) for i in range(self.dp_size)])]
    ppermute x12 -> x13, starting transfers between devices: 11.8 us -> 19.9 us  [half(): return lax.ppermute(array, 'mp', [(i, i ^ 2) for i in range(self.mp_size)])]
    ppermute x24, waiting for transfers between devices: 27.6 us -> 33.9 us  [data(): lax.ppermute(array, 'dp', [(i, i ^ 1 << bit) for i in range(self.dp_size)])]
    pallas_call x2, Pallas kernels: 30.4 us -> 24.5 us  [attention_back(): pl.pallas_call(functools.partial(attention_back_kernel, heads, dim), grid...]
    pallas_call x2, Pallas kernels: 22.6 us -> 18.5 us  [attention(): pl.pallas_call(functools.partial(attention_kernel, heads, dim), out_shape...]
    unnamed x157 -> x163, local copies, waits for them, and re-layouts: 17 us -> 14.9 us
  transfers between devices with their start and end apart: 50 -> 51, of which waited for: 18 -> 21; matrix products, arithmetic and copies ran while one was open for 20% -> 20% of each run, Pallas kernels for 36% -> 34%
where the time goes in v1:
time: 376 us; the launch traced here: 375 us
  Pallas kernels  138 us (37%)
  waiting for transfers between devices  65.2 us (17%)
  starting transfers between devices  63 us (17%)
  local copies, waits for them, and re-layouts  49.1 us (13%)
  other arithmetic  34.1 us (9%)
  matrix products  14.6 us (4%)
  between operations  10.9 us (3%)
    ppermute x24, starting transfers between devices, data(): lax.ppermute(array, 'dp', [(i, i ^ 1 << bit) for i in range(self.dp_size)])  39.6 us
    ppermute x24, waiting for transfers between devices, data(): lax.ppermute(array, 'dp', [(i, i ^ 1 << bit) for i in range(self.dp_size)])  33.9 us
    ppermute x13, waiting for transfers between devices, half(): return lax.ppermute(array, 'mp', [(i, i ^ 2) for i in range(self.mp_size)])  27.4 us
    pallas_call x2, Pallas kernels, attention_back(): pl.pallas_call(functools.partial(attention_back_kernel, heads, dim), grid...  24.5 us
    ppermute x13, starting transfers between devices, half(): return lax.ppermute(array, 'mp', [(i, i ^ 2) for i in range(self.mp_size)])  19.9 us
    pallas_call x1, Pallas kernels, own_mlp(): pl.pallas_call(own_mlp_kernel, grid=(tokens // BLOCK,), out_shape=[struct...  18.7 us
    pallas_call x2, Pallas kernels, attention(): pl.pallas_call(functools.partial(attention_kernel, heads, dim), out_shape...  18.5 us
    pallas_call x2, Pallas kernels, join_sequence(): pl.pallas_call(functools.partial(join_kernel, half_rows, window, len(piec...  17 us
  transfers between devices with their start and end apart: 51, of which 21 were waited for; matrix products, arithmetic and copies ran while one was open for 20% of the time, Pallas kernels for 34%

profile of v1, /device:TPU:0, one launch (start us, length us, event | category | flops | bytes accessed | tf_op | source)
XLA Modules:
  0.0 374.6 jit_solution(1324579745822511130)
XLA Ops:
  10.0 8.9 %heads_own.1 = (bf16[1280,768]{1,0:T(8,128)(2,1)}, bf16[192,1280]{1,0:T(8,128)(2,1)}, bf16[192,1280]{1,0:T(8,128)(2,1)}, bf16[192,1280]{1,0:T(8,128)(2,1)}, bf16...) custom-call(bf16[1280,768]{1,0:T(8,128)(2,1)} %dynamic-slice_bitcast_fusion.1.x_ref, ...), custom_call_target="tpu_custom_call" | custom-call | flops 1132462080 | bytes 7864320 | tf_op jit(solution)/shard_map/heads_own/pallas_call | solution.py:355
  33.4 9.2 %attention.2 = (bf16[192,1280]{1,0:T(8,128)(2,1)}, f32[24,1280]{1,0:T(8,128)}) custom-call(s32[8,128]{1,0:T(8,128)} %copy-done.36, bf16[192,1280]{1,0:T(8,128)(2,1)} %get-tuple-element.150.q_ref, bf16[192,1280]{1,0:T(8,128)(2,1)} %get-tuple-element.151.k_ref, bf16[192,1280]{1,0:T(8,128)(2,1)} %get-tuple-element.152.v_ref, s32[1280,128]{1,0:T(8,128)} %copy-done.18, ...), custom_call_target="tpu_custom_call" | custom-call | flops 754974720 | bytes 1966080 | tf_op jit(solution)/shard_map/attention/pallas_call | solution.py:389
  45.1 7.6 %heads_other.1 = (bf16[192,1280]{1,0:T(8,128)(2,1)}, bf16[192,1280]{1,0:T(8,128)(2,1)}, bf16[192,1280]{1,0:T(8,128)(2,1)}, bf16[192,1280]{1,0:T(8,128)(2,1)}, bf...) custom-call(s32[4]{0:T(128)} %pad_add_fusion.1.spots_ref, ...), custom_call_target="tpu_custom_call" | custom-call | flops 1132462080 | bytes 7864320 | tf_op jit(solution)/shard_map/heads_other/pallas_call | solution.py:372
  59.9 9.3 %attention.3 = (bf16[192,1280]{1,0:T(8,128)(2,1)}, f32[24,1280]{1,0:T(8,128)}) custom-call(s32[8,128]{1,0:T(8,128)} %copy-done.36, bf16[192,1280]{1,0:T(8,128)(2,1)} %get-tuple-element.166.q_ref, bf16[192,1280]{1,0:T(8,128)(2,1)} %get-tuple-element.167.k_ref, bf16[192,1280]{1,0:T(8,128)(2,1)} %get-tuple-element.168.v_ref, s32[1280,128]{1,0:T(8,128)} %copy-done.18, ...), custom_call_target="tpu_custom_call" | custom-call | flops 754974720 | bytes 1966080 | tf_op jit(solution)/shard_map/attention/pallas_call | solution.py:389
  72.9 4.1 %out_project.1.mine_ref = f32[1280,768]{1,0:T(8,128)} custom-call(bf16[192,1280]{1,0:T(8,128)(2,1)S(1)} %copy-done.20, bf16[192,1280]{1,0:T(8,128)(2,1)S(1)} %copy-done.13, f32[192,768]{1,0:T(8,128)S(1)} %copy-done.7, f32[192,768]{1,0:T(8,128)S(1)} %collective-permute-done.8.other_ref.out_other_ref), custom_call_target="tpu_custom_call" | custom-call | flops 754974720 | bytes 5898240 | tf_op jit(solution)/shard_map/out_project/pallas_call | solution.py:404
  84.1 18.7 %mlp_own.1 = (f32[1280,768]{1,0:T(8,128)}, bf16[1280,768]{1,0:T(8,128)(2,1)}, bf16[1280,768]{1,0:T(8,128)(2,1)}, bf16[1280,768]{1,0:T(8,128)(2,1)}, bf16[1280,76...) custom-call(bf16[1280,768]{1,0:T(8,128)(2,1)} %dynamic-slice_bitcast_fusi, ...), custom_call_target="tpu_custom_call" | custom-call | flops 6039797760 | bytes 39321600 | tf_op jit(solution)/shard_map/mlp_own/pallas_call | solution.py:650
  102.8 4.0 %fusion.25 = f32[768,768]{1,0:T(8,128)S(1)} fusion(bf16[1280,768]{1,0:T(8,128)(2,1)} %get-tuple-element.178.a_ref, bf16[1280,768]{1,0:T(8,128)(2,1)} %get-tuple-element.177), kind=kOutput, calls=%fused_computation.93 | convolution fusion | flops 1509949440 | bytes 6291456 | tf_op jit(solution)/shard_map/dot_general | solution.py:33
  116.3 16.1 %mlp_other.1 = (bf16[1280,768]{1,0:T(8,128)(2,1)}, bf16[1280,768]{1,0:T(8,128)(2,1)}, f32[1280,768]{1,0:T(8,128)}, f32[1280,384]{1,0:T(8,128)}, f32[1280,384]{1,0:T(8,128)}, /*index=5*/f32[1,768]{1,0:T(1,128)}) custom-call(s32[4]{0:T(128)} %pad_add_fusion.1.spots_ref, bf16[1280,768]{1,0:T(8,128)(2,1)} %get-tuple-element.178.a_ref, ...), custom_call_target="tpu_custom_call", output_to_operand_aliasing={{2}: (3, {})} | custom-call | flops 6039797760 | bytes 27525120 | tf_op jit(solution)/shard_map/mlp_other/pallas_call | solution.py:688
  136.8 5.5 %collective-permute-done.13 = f32[2,2,96,768]{3,2,1,0:T(8,128)} collective-permute-done((f32[2,2,96,768]{3,2,1,0:T(8,128)}, f32[2,2,96,768]{3,2,1,0:T(8,128)}, u32[]{:S(2)}, u32[]{:S(2)}) %collective-permute-start.13) | collective-permute-done | bytes 1179680 | tf_op jit(solution)/shard_map/ppermute | solution.py:53
  158.2 5.7 %hidden_back.1 = (f32[1280,768]{1,0:T(8,128)S(1)}, bf16[1280,768]{1,0:T(8,128)(2,1)S(1)}, bf16[192,1280]{1,0:T(8,128)(2,1)S(1)}, bf16[192,1280]{1,0:T(8,128)(2,1)S(1)}, f32[4,768]{1,0:T(4,128)S(1)}) custom-call(f32[1280,768]{1,0:T(8,128)S(1)} %copy-done.2, f32[1280,384]{1,0:T(8,128)S(1)} %copy-done.11, f32[1280,384]{1,0:T(8,128)S(1)} %copy-done.12, ...), custom_call_target="tpu_custom_call" | custom-call | flops 754974720 | bytes 21626880 | tf_op jit(solution)/shard_map/hidden_back/pallas_call | solution.py:757
  164.0 12.1 %attention_back.2 = (bf16[768,1280]{1,0:T(8,128)(2,1)S(1)}, bf16[384,1280]{1,0:T(8,128)(2,1)S(1)}, f32[1,1024]{1,0:T(1,128)S(1)}) custom-call(s32[8,128]{1,0:T(8,128)S(1)} %copy-done.37, bf16[192,1280]{1,0:T(8,128)(2,1)S(1)} %copy-done.42, bf16[192,1280]{1,0:T(8,128)(2,1)S(1)} %copy-done.43, bf16[192,1280]{1,0:T(8,128)(2,1)S(1)} %copy-done.44, ...), custom_call_target="tpu_custom_call" | custom-call | flops 1887436800 | bytes 7372800 | tf_op jit(solution)/shard_map/attention_back/pallas_call | solution.py:512
  184.4 12.3 %attention_back.3 = (bf16[768,1280]{1,0:T(8,128)(2,1)S(1)}, bf16[384,1280]{1,0:T(8,128)(2,1)S(1)}, f32[1,1024]{1,0:T(1,128)S(1)}) custom-call(s32[8,128]{1,0:T(8,128)S(1)} %copy-done.37, bf16[192,1280]{1,0:T(8,128)(2,1)S(1)} %copy-done.22, bf16[192,1280]{1,0:T(8,128)(2,1)S(1)} %copy-done.23, ...), custom_call_target="tpu_custom_call", output_to_operand_aliasing={{0}: (13, {}), {1}: (14, {})} | custom-call | flops 1887436800 | bytes 7372800 | tf_op jit(solution)/shard_map/attention_back/pallas_call | solution.py:512
  196.8 8.3 %collective-permute-done.21 = f32[2,96,1536]{2,1,0:T(8,128)S(1)} collective-permute-done((f32[2,96,1536]{2,1,0:T(8,128)S(1)}, f32[2,96,1536]{2,1,0:T(8,128)S(1)}, u32[]{:S(2)}, u32[]{:S(2)}) %collective-permute-start.21) | collective-permute-done | bytes 1179680 | tf_op jit(solution)/shard_map/ppermute | solution.py:53
  220.1 4.3 %last_gradients.1 = (f32[768,384]{1,0:T(8,128)S(1)}, f32[768,384]{1,0:T(8,128)S(1)}, f32[768,768]{1,0:T(8,128)S(1)}) custom-call(bf16[1280,768]{1,0:T(8,128)(2,1)S(1)} %copy-done.10, bf16[1280,768]{1,0:T(8,128)(2,1)S(1)} %get-tuple-element.191.dattn_ref, bf16[768,1280]{1,0:T(8,128)(2,1)S(1)} %get-tuple-element.214.qk_ref, ...), custom_call_target="tpu_custom_call" | custom-call | flops 3019898880 | bytes 11796480 | tf_op jit(solution)/shard_map/last_gradients/pallas_call | solution.py:848
  231.5 6.3 %input_back.1 = (f32[640,384]{1,0:T(8,128)}, f32[640,384]{1,0:T(8,128)}, f32[2,768]{1,0:T(2,128)}) custom-call(s32[1]{0:T(128)} %bitcast.core_ref, f32[1280,768]{1,0:T(8,128)} %copy-done.54, f32[640,768]{1,0:T(8,128)} %collective-permute-done.27.peer_ref, bf16[1280,768]{1,0:T(8,128)(2,1)} %dynamic-slice_bitcast_fusion.1.x_ref, f32[1280,768]{1,0:T(8,128)} %copy-done.6, ...), custom_call_target="tpu_custom_call" | custom-call | bytes 8847360 | tf_op jit(solution)/shard_map/input_back/pallas_call | solution.py:809
  239.8 7.9 %collective-permute-done.34 = f32[2,96,1536]{2,1,0:T(8,128)} collective-permute-done((f32[2,96,1536]{2,1,0:T(8,128)}, f32[2,96,1536]{2,1,0:T(8,128)}, u32[]{:S(2)}, u32[]{:S(2)}) %collective-permute-start.34) | collective-permute-done | bytes 1179680 | tf_op jit(solution)/shard_map/ppermute | solution.py:50
  250.5 4.3 %collective-permute-start.35 = (f32[96,1536]{1,0:T(8,128)}, f32[96,1536]{1,0:T(8,128)}, u32[]{:S(2)}, u32[]{:S(2)}) collective-permute-start(f32[96,1536]{1,0:T(8,128)} %dynamic-slice_bitcast_fusion.7), channel_id=1, source_target_pairs={{0,16},{4,20},{8,24},{12,28},{16,0},{20,4},{24,8},{28,12},{1,17},{... | collective-permute-start | bytes 1769480 | tf_op jit(solution)/shard_map/ppermute | solution.py:53
  263.3 9.7 %collective-permute-done.24 = f32[768,384]{1,0:T(8,128)} collective-permute-done((f32[768,384]{1,0:T(8,128)}, f32[768,384]{1,0:T(8,128)}, u32[]{:S(2)}, u32[]{:S(2)}) %collective-permute-start.24) | collective-permute-done | bytes 1179680 | tf_op jit(solution)/shard_map/ppermute | solution.py:50
  281.6 9.3 %join_sequence.2 = bf16[1,2048,768]{2,1,0:T(8,128)(2,1)} custom-call(s32[3]{0:T(128)} %pad_add_fusion.info_ref, f32[1]{0:T(128)} %constant.142.clone.1.factor_ref, f32[1,768]{1,0:T(1,128)} %get-tuple-element.293.shift_ref, f32[640,768]{1,0:T(8,128)} %copy-done.49, f32[640,768]{1,0:T(8,128)} %copy-done.55, f32[640,384]{1,0:T(8,128)} %copy-done.65, ...), custom_call_target="tpu_custom_call" | custom-call | bytes 11010048 | tf_op jit(solution)/shard_map/join_sequence/pallas_call | solution.py:1010
  298.6 4.9 %collective-permute-done.36 = f32[2,96,384]{2,1,0:T(8,128)S(1)} collective-permute-done((f32[2,96,384]{2,1,0:T(8,128)S(1)}, f32[2,96,384]{2,1,0:T(8,128)S(1)}, u32[]{:S(2)}, u32[]{:S(2)}) %collective-permute-start.36) | collective-permute-done | bytes 294944 | tf_op jit(solution)/shard_map/ppermute | solution.py:50
  310.9 5.0 %collective-permute-start.37 = (f32[96,768]{1,0:T(8,128)S(1)}, f32[96,768]{1,0:T(8,128)S(1)}, u32[]{:S(2)}, u32[]{:S(2)}) collective-permute-start(f32[96,768]{1,0:T(8,128)S(1)} %fusion.16), channel_id=1, source_target_pairs={{0,16},{4,20},{8,24},{12,28},{16,0},{20,4},{24,8},{28,12},{1,17},{... | collective-permute-start | bytes 884744 | tf_op jit(solution)/shard_map/ppermute | solution.py:53
  321.5 7.6 %collective-permute-done.40 = f32[16,768]{1,0:T(8,128)S(1)} collective-permute-done((f32[16,768]{1,0:T(8,128)S(1)}, f32[16,768]{1,0:T(8,128)S(1)}, u32[]{:S(2)}, u32[]{:S(2)}) %collective-permute-start.40) | collective-permute-done | bytes 49184 | tf_op jit(solution)/shard_map/ppermute | solution.py:53
  359.1 4.4 %update.1 = (f32[3,96,192]{2,1,0:T(8,128)}, f32[3,96,192]{2,1,0:T(8,128)}, f32[3,96,192]{2,1,0:T(8,128)}, f32[192,96]{1,0:T(8,128)}, f32[192,96]{1,0:T(8,128)}, ...) custom-call(f32[3]{0:T(128)} %pad_maximum_fusion.6.refs_0_, ...), custom_call_target="tpu_custom_call" | custom-call | bytes 6349056 | tf_op jit(solution)/shard_map/update/pallas_call | solution.py:936
  365.8 7.7 %join_sequence.3 = bf16[1,2048,768]{2,1,0:T(8,128)(2,1)} custom-call(s32[3]{0:T(128)} %pad_add_fusion.info_ref, f32[1]{0:T(128)} %bitcast.52.factor_ref, f32[1,768]{1,0:T(1,128)} %broadcast_in_dim.2.shift_ref, f32[640,384]{1,0:T(8,128)} %get-tuple-element.224.refs_0_, f32[640,384]{1,0:T(8,128)} %collective-permute-done.41.refs_1_, ...), custom_call_target="tpu_custom_call" | custom-call | bytes 11010048 | tf_op jit(solution)/shard_map/join_sequence/pallas_call | solution.py:1010
  (344 shorter events, 170.6 us)
Async XLA Ops:
  21.1 31.6 %collective-permute-start.5 = (f32[2,192,768]{2,1,0:T(8,128)}, f32[2,192,768]{2,1,0:T(8,128)S(1)}, u32[]{:S(2)}, u32[]{:S(2)}) collective-permute-start(f32[2,192,768]{2,1,0:T(8,128)} %fusion.11), channel_id=1, source_target_pairs={{0,2},{1,3},{2,0},{3,1},{4,6},{5,7},{6,4},{7,5},{8,10},{9,11},{10,... | collective-permute-start | bytes 3538952 | tf_op jit(solution)/shard_map/ppermute | solution.py:50
  80.5 34.8 %collective-permute-start.10 = (f32[2,2,96,768]{3,2,1,0:T(8,128)}, f32[2,2,96,768]{3,2,1,0:T(8,128)}, u32[]{:S(2)}, u32[]{:S(2)}) collective-permute-start(f32[2,2,96,768]{3,2,1,0:T(8,128)} %pad_maximum_fusion.1), channel_id=1, source_target_pairs={{0,8},{4,12},{8,0},{12,4},{16,24},{20,28},{24,16},{28,20},{1,9},{5... | collective-permute-start | bytes 3538952 | tf_op jit(solution)/shard_map/ppermute | solution.py:53
  83.3 32.0 %collective-permute-start.11 = (f32[2,2,96,768]{3,2,1,0:T(8,128)}, f32[2,2,96,768]{3,2,1,0:T(8,128)S(1)}, u32[]{:S(2)}, u32[]{:S(2)}) collective-permute-start(f32[2,2,96,768]{3,2,1,0:T(8,128)} %pad_maximum_fusion.2), channel_id=1, source_target_pairs={{0,4},{4,0},{8,12},{12,8},{16,20},{20,16},{24,28},{28,24},{1,5},{5... | collective-permute-start | bytes 3538952 | tf_op jit(solution)/shard_map/ppermute | solution.py:53
  108.0 28.8 %collective-permute-start.14 = (f32[2,2,96,768]{3,2,1,0:T(8,128)}, f32[2,2,96,768]{3,2,1,0:T(8,128)}, u32[]{:S(2)}, u32[]{:S(2)}) collective-permute-start(f32[2,2,96,768]{3,2,1,0:T(8,128)} %dynamic-slice_bitcast_fusion.5), channel_id=1, source_target_pairs={{0,8},{4,12},{8,0},{12,4},{16,24},{20,28},{24,16},{28,20},{1,9},{5... | collective-permute-start | bytes 3538952 | tf_op jit(solution)/shard_map/ppermute | solution.py:53
  114.0 28.3 %collective-permute-start.13 = (f32[2,2,96,768]{3,2,1,0:T(8,128)}, f32[2,2,96,768]{3,2,1,0:T(8,128)}, u32[]{:S(2)}, u32[]{:S(2)}) collective-permute-start(f32[2,2,96,768]{3,2,1,0:T(8,128)} %dynamic-slice_bitcast_fusion.6), channel_id=1, source_target_pairs={{0,4},{4,0},{8,12},{12,8},{16,20},{20,16},{24,28},{28,24},{1,5},{5... | collective-permute-start | bytes 3538952 | tf_op jit(solution)/shard_map/ppermute | solution.py:53
  136.2 22.0 %collective-permute-start.16 = (f32[1280,384]{1,0:T(8,128)}, f32[1280,384]{1,0:T(8,128)S(1)}, u32[]{:S(2)}, u32[]{:S(2)}) collective-permute-start(f32[1280,384]{1,0:T(8,128)} %get-tuple-element.190.mine_right), channel_id=1, source_target_pairs={{0,1},{1,0},{2,3},{3,2},{4,5},{5,4},{6,7},{7,6},{8,9},{9,8},{10,11... | collective-permute-start | bytes 5898248 | tf_op jit(solution)/shard_map/ppermute | solution.py:47
  146.5 29.7 %collective-permute-start.17 = (f32[2,2,96,768]{3,2,1,0:T(8,128)S(1)}, f32[2,2,96,768]{3,2,1,0:T(8,128)S(1)}, u32[]{:S(2)}, u32[]{:S(2)}) collective-permute-start(f32[2,2,96,768]{3,2,1,0:T(8,128)S(1)} %dynamic-slice_bitcast_fusion.4), channel_id=1, source_target_pairs={{0,4},{4,0},{8,12},{12,8},{16,20},{20,16},{24,28},{28,24},{1,5},{5... | collective-permute-start | bytes 3538952 | tf_op jit(solution)/shard_map/ppermute | solution.py:53
  149.8 30.9 %collective-permute-start.18 = (f32[2,2,96,768]{3,2,1,0:T(8,128)S(1)}, f32[2,2,96,768]{3,2,1,0:T(8,128)S(1)}, u32[]{:S(2)}, u32[]{:S(2)}) collective-permute-start(f32[2,2,96,768]{3,2,1,0:T(8,128)S(1)} %dynamic-slice_bitcast_fusion.3), channel_id=1, source_target_pairs={{0,8},{4,12},{8,0},{12,4},{16,24},{20,28},{24,16},{28,20},{1,9},{5... | collective-permute-start | bytes 3538952 | tf_op jit(solution)/shard_map/ppermute | solution.py:53
  154.3 30.0 %collective-permute-start.20 = (f32[640,768]{1,0:T(8,128)S(1)}, f32[640,768]{1,0:T(8,128)S(1)}, u32[]{:S(2)}, u32[]{:S(2)}) collective-permute-start(f32[640,768]{1,0:T(8,128)S(1)} %get-tuple-element.227.refs_0_.refs_4_), channel_id=1, source_target_pairs={{0,1},{1,0},{2,3},{3,2},{4,5},{5,4},{6,7},{7,6},{8,9},{9,8},{10,11... | collective-permute-start | bytes 5898248 | tf_op jit(solution)/shard_map/ppermute | solution.py:47
  157.6 26.7 %collective-permute-start.19 = (f32[640,384]{1,0:T(8,128)}, f32[640,384]{1,0:T(8,128)S(1)}, u32[]{:S(2)}, u32[]{:S(2)}) collective-permute-start(f32[640,384]{1,0:T(8,128)} %slice.118), channel_id=1, source_target_pairs={{0,2},{1,3},{2,0},{3,1},{4,6},{5,7},{6,4},{7,5},{8,10},{9,11},{10,... | collective-permute-start | bytes 2949128 | tf_op jit(solution)/shard_map/ppermute | solution.py:50
  176.5 28.6 %collective-permute-start.21 = (f32[2,96,1536]{2,1,0:T(8,128)S(1)}, f32[2,96,1536]{2,1,0:T(8,128)S(1)}, u32[]{:S(2)}, u32[]{:S(2)}) collective-permute-start(f32[2,96,1536]{2,1,0:T(8,128)S(1)} %fusion.10), channel_id=1, source_target_pairs={{0,8},{4,12},{8,0},{12,4},{16,24},{20,28},{24,16},{28,20},{1,9},{5... | collective-permute-start | bytes 3538952 | tf_op jit(solution)/shard_map/ppermute | solution.py:53
  181.1 27.4 %collective-permute-start.22 = (f32[2,96,1536]{2,1,0:T(8,128)S(1)}, f32[2,96,1536]{2,1,0:T(8,128)S(1)}, u32[]{:S(2)}, u32[]{:S(2)}) collective-permute-start(f32[2,96,1536]{2,1,0:T(8,128)S(1)} %fusion.5), channel_id=1, source_target_pairs={{0,4},{4,0},{8,12},{12,8},{16,20},{20,16},{24,28},{28,24},{1,5},{5... | collective-permute-start | bytes 3538952 | tf_op jit(solution)/shard_map/ppermute | solution.py:53
  181.3 29.4 %collective-permute-start.23 = (f32[640,384]{1,0:T(8,128)S(1)}, f32[640,384]{1,0:T(8,128)S(1)}, u32[]{:S(2)}, u32[]{:S(2)}) collective-permute-start(f32[640,384]{1,0:T(8,128)S(1)} %slice.101), channel_id=1, source_target_pairs={{0,2},{1,3},{2,0},{3,1},{4,6},{5,7},{6,4},{7,5},{8,10},{9,11},{10,... | collective-permute-start | bytes 2949128 | tf_op jit(solution)/shard_map/ppermute | solution.py:50
  218.6 29.1 %collective-permute-start.34 = (f32[2,96,1536]{2,1,0:T(8,128)}, f32[2,96,1536]{2,1,0:T(8,128)}, u32[]{:S(2)}, u32[]{:S(2)}) collective-permute-start(f32[2,96,1536]{2,1,0:T(8,128)} %pad_maximum_fusion.3), channel_id=1, source_target_pairs={{0,2},{1,3},{2,0},{3,1},{4,6},{5,7},{6,4},{7,5},{8,10},{9,11},{10,... | collective-permute-start | bytes 3538952 | tf_op jit(solution)/shard_map/ppermute | solution.py:50
  227.1 27.9 %collective-permute-start.25 = (f32[2,2,96,768]{3,2,1,0:T(8,128)}, f32[2,2,96,768]{3,2,1,0:T(8,128)}, u32[]{:S(2)}, u32[]{:S(2)}) collective-permute-start(f32[2,2,96,768]{3,2,1,0:T(8,128)} %dynamic-slice_bitcast_fusion.2), channel_id=1, source_target_pairs={{0,4},{4,0},{8,12},{12,8},{16,20},{20,16},{24,28},{28,24},{1,5},{5... | collective-permute-start | bytes 3538952 | tf_op jit(solution)/shard_map/ppermute | solution.py:53
  231.4 41.6 %collective-permute-start.24 = (f32[768,384]{1,0:T(8,128)}, f32[768,384]{1,0:T(8,128)}, u32[]{:S(2)}, u32[]{:S(2)}) collective-permute-start(f32[768,384]{1,0:T(8,128)} %copy-done.41), channel_id=1, source_target_pairs={{0,2},{1,3},{2,0},{3,1},{4,6},{5,7},{6,4},{7,5},{8,10},{9,11},{10,... | collective-permute-start | bytes 3538952 | tf_op jit(solution)/shard_map/ppermute | solution.py:50
  237.8 59.2 %collective-permute-start.30 = (f32[640,384]{1,0:T(8,128)}, f32[640,384]{1,0:T(8,128)}, u32[]{:S(2)}, u32[]{:S(2)}) collective-permute-start(f32[640,384]{1,0:T(8,128)} %get-tuple-element.224.refs_0_), channel_id=1, source_target_pairs={{0,2},{1,3},{2,0},{3,1},{4,6},{5,7},{6,4},{7,5},{8,10},{9,11},{10,... | collective-permute-start | bytes 2949128 | tf_op jit(solution)/shard_map/ppermute | solution.py:50
  250.5 43.5 %collective-permute-start.35 = (f32[96,1536]{1,0:T(8,128)}, f32[96,1536]{1,0:T(8,128)}, u32[]{:S(2)}, u32[]{:S(2)}) collective-permute-start(f32[96,1536]{1,0:T(8,128)} %dynamic-slice_bitcast_fusion.7), channel_id=1, source_target_pairs={{0,16},{4,20},{8,24},{12,28},{16,0},{20,4},{24,8},{28,12},{1,17},{... | collective-permute-start | bytes 1769480 | tf_op jit(solution)/shard_map/ppermute | solution.py:53
  258.4 35.7 %collective-permute-start.33 = (f32[2,96,768]{2,1,0:T(8,128)}, f32[2,96,768]{2,1,0:T(8,128)}, u32[]{:S(2)}, u32[]{:S(2)}) collective-permute-start(f32[2,96,768]{2,1,0:T(8,128)} %dynamic-slice_bitcast_fusion.9), channel_id=1, source_target_pairs={{0,8},{4,12},{8,0},{12,4},{16,24},{20,28},{24,16},{28,20},{1,9},{5... | collective-permute-start | bytes 1769480 | tf_op jit(solution)/shard_map/ppermute | solution.py:53
  315.9 25.2 %collective-permute-start.44 = (f32[640,384]{1,0:T(8,128)}, f32[640,384]{1,0:T(8,128)S(1)}, u32[]{:S(2)}, u32[]{:S(2)}) collective-permute-start(f32[640,384]{1,0:T(8,128)} %get-tuple-element.248.refs_4_), channel_id=1, source_target_pairs={{0,2},{1,3},{2,0},{3,1},{4,6},{5,7},{6,4},{7,5},{8,10},{9,11},{10,... | collective-permute-start | bytes 2949128 | tf_op jit(solution)/shard_map/ppermute | solution.py:50
  316.5 47.7 %collective-permute-start.41 = (f32[640,384]{1,0:T(8,128)}, f32[640,384]{1,0:T(8,128)}, u32[]{:S(2)}, u32[]{:S(2)}) collective-permute-start(f32[640,384]{1,0:T(8,128)} %get-tuple-element.224.refs_0_), channel_id=1, source_target_pairs={{0,1},{1,0},{2,3},{3,2},{4,5},{5,4},{6,7},{7,6},{8,9},{9,8},{10,11... | collective-permute-start | bytes 2949128 | tf_op jit(solution)/shard_map/ppermute | solution.py:47
  316.5 47.7 %collective-permute-start.43 = (f32[640,384]{1,0:T(8,128)}, f32[640,384]{1,0:T(8,128)}, u32[]{:S(2)}, u32[]{:S(2)}) collective-permute-start(f32[640,384]{1,0:T(8,128)} %get-tuple-element.248.refs_4_), channel_id=1, source_target_pairs={{0,1},{1,0},{2,3},{3,2},{4,5},{5,4},{6,7},{7,6},{8,9},{9,8},{10,11... | collective-permute-start | bytes 2949128 | tf_op jit(solution)/shard_map/ppermute | solution.py:47
  329.0 35.2 %collective-permute-start.42 = (f32[640,384]{1,0:T(8,128)}, f32[640,384]{1,0:T(8,128)S(1)}, u32[]{:S(2)}, u32[]{:S(2)}) collective-permute-start(f32[640,384]{1,0:T(8,128)} %collective-permute-done.30.refs_2_), channel_id=1, source_target_pairs={{0,1},{1,0},{2,3},{3,2},{4,5},{5,4},{6,7},{7,6},{8,9},{9,8},{10,11... | collective-permute-start | bytes 2949128 | tf_op jit(solution)/shard_map/ppermute | solution.py:47
  341.1 23.2 %collective-permute-start.47 = (f32[640,384]{1,0:T(8,128)S(1)}, f32[640,384]{1,0:T(8,128)}, u32[]{:S(2)}, u32[]{:S(2)}) collective-permute-start(f32[640,384]{1,0:T(8,128)S(1)} %collective-permute-done.44.refs_6_), channel_id=1, source_target_pairs={{0,1},{1,0},{2,3},{3,2},{4,5},{5,4},{6,7},{7,6},{8,9},{9,8},{10,11... | collective-permute-start | bytes 2949128 | tf_op jit(solution)/shard_map/ppermute | solution.py:47
  (107 other events, 767.7 us)
